TPU v7x, 32 devices: a whole 2x2x4 slice. The times are simulated.
32 devices in a mesh: tok: 8 (over z, x), feat: 4 (over y, core).
Axes of the slice: x: 2, y: 2, z: 4, core: 2. Of those that a mesh axis runs over, the one named last changes fastest.
Arguments:
- activations: bfloat16 [8192, 28672], P('tok', 'feat'), may hold values from -6 to 6
- out_grads: bfloat16 [8192, 8192], P('tok', 'feat'), may hold values from -6 to 6
- proj_in: bfloat16 [28672, 256], P('feat'), may hold values from -0.03125 to 0.03125
- proj_out: bfloat16 [8192, 256], P('feat'), may hold values from -0.0625 to 0.0625
- left_factor: float32 [256, 256], replicated, may hold values from -0.375 to 0.375
- right_factor: float32 [256, 256], replicated, may hold values from -0.375 to 0.375
- seq_lengths: int32 [64], replicated, may hold values from 1 to 255, as said below
- seq_slots: int32 [64], replicated, may hold values from 0 to 63, each once
- stored_grads: float32 [256, 65536], P('tok', 'feat'), may hold values from -0.375 to 0.375
Outputs:
- scores: float32 [256, 64], P(('tok', 'feat'))
- seq_grads: float32 [64, 65536], P('tok', 'feat')
Inputs may be any that keep to these rules, and one draw needn't show every extreme that they name: `seq_lengths`: the lengths sum to 8192. Sequence s starts within tokens s * (128) to (s + 1) * 128 - 1, the first at token 0, so exactly 8 sequences start in the tokens of each index of tok, at most 9 sequences meet them (exactly that many at index 1), and a sequence meets the tokens of at most two indices. The longest is exactly 255. `seq_slots`: every slot is used by exactly one sequence.
All inputs are finite; a program needn't handle non-finite values.
Results may differ from a plain program's by a relative error of at most 0.0003.
Values sent between devices are 32-bit elements; how exact they have to be, the bound alone decides.
A program may use at most 128 MiB of HBM per device.

v0:
```python
import jax
import jax.numpy as jnp
from jax import lax
from jax.sharding import PartitionSpec as P


def shifted(value, axis, steps):
    count = lax.axis_size(axis)
    first, last = (max(0, -steps), min(count, count - steps))
    return lax.ppermute(value, axis, [(source, source + steps) for source in range(first, last)])


def body(
    activations,
    out_grads,
    proj_in,
    proj_out,
    left_factor,
    right_factor,
    seq_lengths,
    seq_slots,
    stored_grads,
):
    highest = lax.Precision.HIGHEST
    feat_count = lax.axis_size("feat")
    tok_count = lax.axis_size("tok")
    rank = right_factor.shape[0]
    share = rank // feat_count
    tok_rows = activations.shape[0]
    seq_count = seq_lengths.shape[0]
    seq_local = seq_count // tok_count
    feat_index = lax.axis_index("feat")
    tok_index = lax.axis_index("tok")
    in_part = jnp.dot(activations, proj_in, preferred_element_type=jnp.float32)
    out_part = jnp.dot(out_grads, proj_out, preferred_element_type=jnp.float32)
    in_total, out_total = lax.psum((in_part, out_part), "feat")
    left_rows = lax.dynamic_slice_in_dim(left_factor, feat_index * share, share, 0)
    right_side = jnp.dot(in_total, right_factor, precision=highest)
    left_side = jnp.dot(out_total, left_rows.T, precision=highest)
    ends = jnp.cumsum(seq_lengths)
    starts = ends - seq_lengths
    places = tok_index * tok_rows + jnp.arange(tok_rows, dtype=jnp.int32)
    near_count = seq_local + 1
    zero_head = jnp.zeros((1,), jnp.int32)
    pad_starts = jnp.concatenate([zero_head, starts])
    pad_ends = jnp.concatenate([zero_head, ends])
    pad_lengths = jnp.concatenate([jnp.ones((1,), jnp.int32), seq_lengths])
    near_starts = lax.dynamic_slice_in_dim(pad_starts, tok_index * seq_local, near_count, 0)
    near_ends = lax.dynamic_slice_in_dim(pad_ends, tok_index * seq_local, near_count, 0)
    near_lengths = lax.dynamic_slice_in_dim(pad_lengths, tok_index * seq_local, near_count, 0)
    near_inside = (
        (places[:, None] >= near_starts[None, :]) & (places[:, None] < near_ends[None, :])
    ).astype(jnp.float32)
    near_weights = near_inside / near_lengths.astype(jnp.float32)[None, :]
    spread = (near_weights[:, :, None] * left_side[:, None, :]).reshape(
        tok_rows, near_count * share
    )
    result = lax.dot_general(spread, right_side, (((0,), (0,)), ((), ())), precision=highest)
    near_part = result.reshape(near_count, share * rank)
    incoming = shifted(near_part[0], "tok", -1)
    finished = near_part[1:].at[seq_local - 1].add(incoming)
    by_sequence = lax.all_gather(finished, "tok", axis=0, tiled=True)
    numbers = jnp.arange(seq_count, dtype=jnp.int32)
    inverse = jnp.sum(
        jnp.where(seq_slots[:, None] == numbers[None, :], numbers[:, None], 0), axis=0
    )
    all_grads = jnp.take(by_sequence, inverse, axis=0)
    own_rows = lax.dynamic_slice_in_dim(all_grads, tok_index * seq_local, seq_local, 0)
    scores = lax.psum_scatter(
        lax.dot_general(stored_grads, all_grads, (((1,), (1,)), ((), ())), precision=highest),
        "feat",
        scatter_dimension=0,
        tiled=True,
    )
    return (scores, own_rows)


def solution(mesh):
    placed = (
        P("tok", "feat"),
        P("tok", "feat"),
        P("feat", None),
        P("feat", None),
        P(),
        P(),
        P(),
        P(),
        P("tok", "feat"),
    )
    return jax.shard_map(
        body,
        mesh=mesh,
        in_specs=placed,
        out_specs=(P(("tok", "feat"), None), P("tok", "feat")),
        check_vma=False,
    )
```

profile of v0, /device:TPU:0, one launch (start us, length us, event | category | flops | bytes accessed | tf_op | source)
XLA Modules:
  0.0 194.6 jit_solution(6945317668369142815)
XLA Ops:
  7.2 11.3 %fusion.5 = f32[1024,256]{1,0:T(8,128)} fusion(bf16[1024,7168]{1,0:T(8,128)(2,1)} %param.11, bf16[7168,256]{1,0:T(8,128)(2,1)} %param.13), kind=kOutput, calls=%fused_computation.25 | convolution fusion | flops 3758096384 | bytes 19398656 | tf_op jit(solution)/shard_map/dot_general | solution.py:34
  18.6 2.3 %fusion.4 = f32[1024,256]{1,0:T(8,128)} fusion(bf16[1024,2048]{1,0:T(8,128)(2,1)S(1)} %copy-done.4, bf16[2048,256]{1,0:T(8,128)(2,1)S(1)} %copy-done.5), kind=kOutput, calls=%fused_computation.24 | convolution fusion | flops 1073741824 | bytes 6291456 | tf_op jit(solution)/shard_map/dot_general | solution.py:35
  20.9 0.1 copy.15
  21.0 0.1 reduce-window.9
  21.1 0.1 reduce.2
  21.7 53.5 %all-reduce.4.cloned.1.call-done = (f32[1024,256]{1,0:T(8,128)}, f32[1024,256]{1,0:T(8,128)}) async-done(((f32[1024,256]{1,0:T(8,128)}, f32[1024,256]{1,0:T(8,128)}), (f32[1024,256]{1,0:T(8,128)}, f32[1024,256]{1,0:T(8,128)})) %all-reduce.4.cloned.1.call-update) | async-done | bytes 2097168 | tf_op jit(solution)/shard_map/psum | solution.py:36
  75.2 2.2 %fusion.6 = f32[1024,256]{1,0:T(8,128)S(1)} fusion(f32[1024,256]{1,0:T(8,128)} %get-tuple-element.15, f32[256,256]{1,0:T(8,128)S(1)} %copy-done.2), kind=kOutput, calls=%fused_computation.26 | convolution fusion | flops 805306368 | bytes 2359296 | tf_op jit(solution)/shard_map/dot_general | solution.py:38
  77.4 2.4 %fusion = f32[1024,64]{0,1:T(8,128)S(1)} fusion(f32[1024,256]{1,0:T(8,128)} %get-tuple-element.14, f32[256,256]{1,0:T(8,128)} %param.15, s32[]{:T(128)S(6)} %select_n.38), kind=kOutput, calls=%fused_computation.6 | convolution fusion | flops 201326592 | bytes 1376260 | tf_op jit(solution)/shard_map/dot_general | solution.py:39
  79.8 0.3 broadcast_multiply_fusion
  80.1 2.0 %fusion.7 = f32[576,256]{1,0:T(8,128)S(1)} fusion(f32[1024,576]{0,1:T(8,128)S(1)} %bitcast.27, f32[1024,256]{1,0:T(8,128)S(1)} %fusion.6), kind=kOutput, calls=%fused_computation.27 | convolution fusion | flops 1811939328 | bytes 3997696 | tf_op jit(solution)/shard_map/dot_general | solution.py:58
  82.2 1.5 collective-permute-start
  83.7 0.1 slice.30
  83.9 4.5 %collective-permute-done = f32[16384]{0:T(1024)S(1)} collective-permute-done((f32[16384]{0:T(1024)S(1)}, f32[16384]{0:T(1024)S(1)}, u32[]{:S(2)}, u32[]{:S(2)}) %collective-permute-start) | collective-permute-done | bytes 65568 | tf_op jit(solution)/shard_map/ppermute | solution.py:10
  88.3 0.5 scatter-add.4
  88.9 0.8 copy-done.1
  89.7 0.6 dynamic-slice.8
  90.9 0.1 select_reduce_fusion
  91.1 71.6 %all-gather.2.cloned.1.call-done = f32[64,16384]{1,0:T(8,128)} async-done(((f32[8,16384]{1,0:T(8,128)}), f32[64,16384]{1,0:T(8,128)}) %all-gather.2.cloned.1.call-update) | async-done | bytes 4194320 | tf_op jit(solution)/shard_map/all_gather | solution.py:62
  162.7 7.6 %gather_fusion = f32[64,16384]{1,0:T(8,128)} fusion(f32[64,16384]{1,0:T(8,128)} %all-gather.2.cloned.1.call-done, s32[1024]{0:T(1024)S(1)} %pad_clamp_fusion), kind=kCustom, calls=%fused_computation | custom fusion | bytes 8388864 | tf_op jit(solution)/shard_map/jit(_take)/gather | solution.py:67
  170.3 2.6 %broadcast_select_fusion = f32[64,16384]{1,0:T(8,128)S(1)} fusion(f32[64,16384]{1,0:T(8,128)} %gather_fusion, pred[64]{0:T(512)(128)(4,1)S(1)} %compare_and_fusion), kind=kLoop, calls=%fused_computation.1 | loop fusion | flops 1048576 | bytes 8388672 | tf_op jit(solution)/shard_map/jit(_take)/select_n | solution.py:67
  172.9 3.4 %convolution_bitcast_fusion = f32[32,64]{1,0:T(8,128)S(1)} fusion(f32[64,16384]{1,0:T(8,128)S(1)} %broadcast_select_fusion, f32[32,16384]{1,0:T(8,128)S(1)} %copy-done), kind=kOutput, calls=%fused_computation.3 | convolution fusion | flops 402653184 | bytes 6299648 | tf_op jit(solution)/shard_map/dot_general | solution.py:70
  176.2 0.8 constant_dynamic-slice_fusion.1
  177.1 10.1 %all-reduce = f32[32,64]{1,0:T(8,128)S(1)} all-reduce(f32[32,64]{1,0:T(8,128)S(1)} %convolution_bitcast_fusion), channel_id=2, replica_groups=mesh['tok'=8,'feat'=4] {'feat'}, use_global_device_ids=true, to_apply=%region_4.5.clone | all-reduce | flops 2048 | bytes 16384
  187.2 0.6 constant_dynamic-slice_fusion
  (35 shorter events, 0.8 us)
Async XLA Ops:
  7.2 165.7 %copy-start = (f32[32,16384]{1,0:T(8,128)S(1)}, f32[32,16384]{1,0:T(8,128)}, u32[]{:S(2)}) copy-start(f32[32,16384]{1,0:T(8,128)} %param.19) | copy-start | bytes 6291460
  7.2 11.4 %copy-start.5 = (bf16[2048,256]{1,0:T(8,128)(2,1)S(1)}, bf16[2048,256]{1,0:T(8,128)(2,1)}, u32[]{:S(2)}) copy-start(bf16[2048,256]{1,0:T(8,128)(2,1)} %param.14) | copy-start | bytes 3145732
  7.2 68.0 %all-reduce.4.cloned.1.call-start = ((), (), s32[]{:S(2)}) async-start(), calls=%async_computation.1 | async-start | bytes 4194304 | tf_op jit(solution)/shard_map/psum | solution.py:36
  7.2 11.3 %copy-start.4 = (bf16[1024,2048]{1,0:T(8,128)(2,1)S(1)}, bf16[1024,2048]{1,0:T(8,128)(2,1)}, u32[]{:S(2)}) copy-start(bf16[1024,2048]{1,0:T(8,128)(2,1)} %param.12) | copy-start | bytes 12582916
  18.5 2.4 %copy-start.3 = (s32[64]{0:T(128)S(1)}, s32[64]{0:T(128)}, u32[]{:S(2)}) copy-start(s32[64]{0:T(128)} %param.17) | copy-start | bytes 772
  18.6 56.6 %copy-start.2 = (f32[256,256]{1,0:T(8,128)S(1)}, f32[256,256]{1,0:T(8,128)}, u32[]{:S(2)}) copy-start(f32[256,256]{1,0:T(8,128)} %param.16) | copy-start | bytes 786436
  20.8 141.8 %all-gather.2.cloned.1.call-start = ((), (), s32[]{:S(2)}) async-start(), calls=%async_computation | async-start | bytes 4718592 | tf_op jit(solution)/shard_map/all_gather | solution.py:62
  80.1 9.6 %copy-start.7 = (u32[32]{0:T(128)S(1)}, u32[32]{0:T(128)}, u32[]{:S(2)}) copy-start(u32[32]{0:T(128)} %constant.72) | copy-start | bytes 388
  80.1 10.8 %copy-start.6 = (s32[64]{0:T(128)S(1)}, s32[64]{0:T(128)}, u32[]{:S(2)}) copy-start(s32[64]{0:T(128)} %param.18) | copy-start | bytes 772
  82.2 6.2 %collective-permute-start = (f32[16384]{0:T(1024)S(1)}, f32[16384]{0:T(1024)S(1)}, u32[]{:S(2)}, u32[]{:S(2)}) collective-permute-start(f32[16384]{0:T(1024)S(1)} %bitcast.30), channel_id=1, source_target_pairs={{4,0},{8,4},{12,8},{16,12},{20,16},{24,20},{28,24},{5,1},{9,5},{13... | collective-permute-start | bytes 196616 | tf_op jit(solution)/shard_map/ppermute | solution.py:10
  88.8 0.8 copy-start.1
Sparse Core Ops, SparseCore 0:
  21.0 54.1 all-reduce.3
  89.8 72.8 all-gather.1
where the time goes:
time: 195 us
  waiting for transfers between devices  130 us (67%)
  matrix products  23.5 us (12%)
  between operations  14.9 us (8%)
  local copies, waits for them, and re-layouts  11.4 us (6%)
  blocking collectives  10.1 us (5%)
  other arithmetic  3.5 us (2%)
    all_gather x1, waiting for transfers between devices, body(): by_sequence = lax.all_gather(finished, 'tok', axis=0, tiled=True)  71.6 us
    psum x1, waiting for transfers between devices, body(): in_total, out_total = lax.psum((in_part, out_part), 'feat')  53.5 us
    dot_general x1, matrix products, body(): in_part = jnp.dot(activations, proj_in, preferred_element_type=jnp.float32)  11.3 us
    unnamed x1, blocking collectives  10.1 us
    gather x1, local copies, waits for them, and re-layouts, body(): all_grads = jnp.take(by_sequence, inverse, axis=0)  7.64 us
    ppermute x1, waiting for transfers between devices, shifted(): lax.ppermute(value, axis, [(source, source + steps) for source in range(f...  4.49 us
  transfers between devices with their start and end apart: 3, of which 3 were waited for; matrix products, arithmetic and copies ran while one was open for 1% of the time, Pallas kernels for 0%

commit v1 on v0

v1 whole, which is shorter than its diff:
```python
import functools

import jax
import jax.numpy as jnp
from jax import lax
from jax.experimental import pallas as pl
from jax.experimental.pallas import tpu as pltpu
from jax.sharding import PartitionSpec as P

MESH = pl.DeviceIdType.MESH
VMEM = pl.BlockSpec(memory_space=pltpu.VMEM)


def remote(src, dst, send_sem, recv_sem, tok, feat):
    return pltpu.make_async_remote_copy(
        src_ref=src, dst_ref=dst, send_sem=send_sem, recv_sem=recv_sem,
        device_id=(tok, feat), device_id_type=MESH,
    )


def greet(barrier, tok, feat):
    pl.semaphore_signal(barrier, inc=1, device_id=(tok, feat), device_id_type=MESH)


def sum_kernel(chips, rows, *refs):
    ins, outs, first, held, second = refs[0:2], refs[2:4], refs[4:6], refs[6:8], refs[8:10]
    send1, recv1, send2, recv2 = refs[10:14]
    tok, feat = lax.axis_index("tok"), lax.axis_index("feat")
    pair, core = feat // 2, feat % 2
    mate = pair * 2 + (1 - core)
    barrier = pltpu.get_barrier_semaphore()
    greet(barrier, tok, mate)
    for step in range(1, chips):
        greet(barrier, tok, ((pair + step) % chips) * 2 + core)
    pl.semaphore_wait(barrier, chips)

    def block(ref, step, side):
        owner = ((pair + step) % chips) * 2 + side
        return ref.at[pl.ds(pl.multiple_of(owner * rows, rows), rows)]

    order = [(step, k) for step in list(range(1, chips)) + [0] for k in range(2)]
    copies1 = {}
    for step, k in order:
        copies1[step, k] = remote(
            block(ins[k], step, 1 - core), first[k].at[step],
            send1.at[k, step], recv1.at[k, step], tok, mate,
        )
        copies1[step, k].start()
    copies2 = {}
    for step, k in order:
        copies1[step, k].wait_recv()
        held[k][step] = block(ins[k], step, core)[...] + first[k][step]
        if step:
            copies2[step, k] = remote(
                held[k].at[step], second[k].at[step],
                send2.at[k, step], recv2.at[k, step], tok, ((pair + step) % chips) * 2 + core,
            )
            copies2[step, k].start()
    for k in range(2):
        total = held[k][0]
        for step in range(1, chips):
            copies2[step, k].wait_recv()
            total += second[k][step]
        outs[k][...] = total
    for copy in list(copies1.values()) + list(copies2.values()):
        copy.wait_send()


def gather_kernel(feats, groups, local, height, near, offsets, part, out, recv, sends, recvs, usend, urecv):
    tok, feat = lax.axis_index("tok"), lax.axis_index("feat")
    group, half = tok // 2, tok % 2
    count = 2 * feats
    me = half * feats + feat
    barrier = pltpu.get_barrier_semaphore()
    for step in range(1, count):
        peer = (me + step) % count
        greet(barrier, group * 2 + peer // feats, peer % feats)

    @pl.when(group > 0)
    def _():
        greet(barrier, tok - 2, feat)

    @pl.when(group < groups - 1)
    def _():
        greet(barrier, tok + 2, feat)

    ends = (group > 0).astype(jnp.int32) + (group < groups - 1).astype(jnp.int32)
    pl.semaphore_wait(barrier, count - 1 + ends)
    spacing, rows = offsets
    copies = {}
    for step in range(1, count):
        peer = (me + step) % count
        first = pl.multiple_of(((peer % feats) * 2 + peer // feats) * height, height)
        copies[step] = remote(
            part.at[:, pl.ds(first, height), :], recv.at[step],
            sends.at[step], recvs.at[step], group * 2 + peer // feats, peer % feats,
        )
        copies[step].start()
    out[group] = jnp.zeros(out.shape[1:], out.dtype)
    mine = pl.multiple_of((feat * 2 + half) * height, height)
    for step in range(count):
        source = (me + count - step) % count
        base = (source // feats) * local + ((source % feats) * rows) // spacing
        if step:
            copies[step].wait_recv()
        for k in range(near):
            block = recv[step, k] if step else part[k, pl.ds(mine, height), :]
            out[group, base + k] += block

    def up(step):
        at = jnp.maximum(group - step, 0)
        return remote(out.at[at], out.at[at], usend.at[0, step], urecv.at[0, step], tok + 2, feat)

    def down(step):
        at = jnp.minimum(group + step, groups - 1)
        return remote(out.at[at], out.at[at], usend.at[1, step], urecv.at[1, step], tok - 2, feat)

    def each(move, what, when):
        @pl.when(when)
        def _():
            getattr(move, what)()

    for step in range(groups - 1):
        ups = (group - step >= 0) & (group + 1 < groups)
        downs = (group + step < groups) & (group - 1 >= 0)
        each(up(step), "start", ups)
        each(down(step), "start", downs)
        each(up(step), "wait_recv", group - 1 - step >= 0)
        each(down(step), "wait_recv", group + 1 + step < groups)
    for step in range(groups - 1):
        each(up(step), "wait_send", (group - step >= 0) & (group + 1 < groups))
        each(down(step), "wait_send", (group + step < groups) & (group - 1 >= 0))
    for step in range(1, count):
        copies[step].wait_send()


def last_kernel(feats, rows, scores, rows_out, total, recv, sends, recvs, rsend, rrecv):
    tok, feat = lax.axis_index("tok"), lax.axis_index("feat")
    group, half = tok // 2, tok % 2
    count = 2 * feats
    me = half * feats + feat
    barrier = pltpu.get_barrier_semaphore()
    for step in range(1, count):
        peer = (me + step) % count
        greet(barrier, group * 2 + peer // feats, peer % feats)
    pl.semaphore_wait(barrier, count - 1)
    trade = remote(rows, rows_out, rsend, rrecv, group * 2 + 1 - half, feat)
    trade.start()
    copies = {}
    for step in range(1, count):
        peer = (me + step) % count
        copies[step] = remote(
            scores.at[peer], recv.at[step], sends.at[step], recvs.at[step],
            group * 2 + peer // feats, peer % feats,
        )
        copies[step].start()
    summed = scores[me]
    for step in range(1, count):
        copies[step].wait_recv()
        summed += recv[step]
    total[...] = summed
    trade.wait()
    for step in range(1, count):
        copies[step].wait_send()


def body(
    activations,
    out_grads,
    proj_in,
    proj_out,
    left_factor,
    right_factor,
    seq_lengths,
    seq_slots,
    stored_grads,
):
    highest = lax.Precision.HIGHEST
    f32 = jnp.float32
    dma = pltpu.SemaphoreType.DMA
    feats, toks = lax.axis_size("feat"), lax.axis_size("tok")
    chips, groups, count = feats // 2, toks // 2, 2 * feats
    rank = right_factor.shape[0]
    tok_rows = activations.shape[0]
    seq_count = seq_lengths.shape[0]
    local = seq_count // toks
    spacing = tok_rows // local
    rows = tok_rows // feats
    height = rank // count
    near = max(rows // spacing, 1) + 1
    feat, tok = lax.axis_index("feat"), lax.axis_index("tok")
    half = tok % 2
    store_rows, width = stored_grads.shape
    wide = width // 2

    kept = lax.dynamic_slice_in_dim(stored_grads, half * wide, wide, 1)
    given = lax.dynamic_slice_in_dim(stored_grads, (1 - half) * wide, wide, 1)
    taken = lax.ppermute(given, "tok", [(t, t + 1 - 2 * (t % 2)) for t in range(toks)])

    out_part = jnp.dot(out_grads, proj_out, preferred_element_type=f32)
    in_part = jnp.dot(activations, proj_in, preferred_element_type=f32)
    out_total, in_total = pl.pallas_call(
        functools.partial(sum_kernel, chips, rows),
        out_shape=[jax.ShapeDtypeStruct((rows, rank), f32)] * 2,
        in_specs=[VMEM] * 2,
        out_specs=[VMEM] * 2,
        scratch_shapes=[pltpu.VMEM((chips, rows, rank), f32)] * 6 + [dma((2, chips))] * 4,
        compiler_params=pltpu.CompilerParams(collective_id=0, has_side_effects=True),
        name="sum_rows",
    )(out_part, in_part)
    right_side = jnp.dot(in_total, right_factor, precision=highest)
    left_side = jnp.dot(out_total, left_factor.T, precision=highest)

    ends = jnp.cumsum(seq_lengths)
    starts = ends - seq_lengths
    places = tok * tok_rows + feat * rows + jnp.arange(rows, dtype=jnp.int32)
    base = tok * local + (feat * rows) // spacing
    zero = jnp.zeros((1,), jnp.int32)
    near_starts = lax.dynamic_slice_in_dim(jnp.concatenate([zero, starts]), base, near, 0)
    near_ends = lax.dynamic_slice_in_dim(jnp.concatenate([zero, ends]), base, near, 0)
    near_lengths = lax.dynamic_slice_in_dim(jnp.concatenate([zero + 1, seq_lengths]), base, near, 0)
    inside = (
        (places[:, None] >= near_starts[None, :]) & (places[:, None] < near_ends[None, :])
    ).astype(f32)
    weights = inside / near_lengths.astype(f32)[None, :]
    spread = jnp.concatenate([weights[:, k : k + 1] * left_side for k in range(near)], axis=1)
    part = lax.dot_general(spread, right_side, (((0,), (0,)), ((), ())), precision=highest)

    blocks = 2 * local + 1
    gathered = pl.pallas_call(
        functools.partial(gather_kernel, feats, groups, local, height, near, (spacing, rows)),
        out_shape=jax.ShapeDtypeStruct((groups, blocks, height, rank), f32),
        in_specs=[VMEM],
        out_specs=VMEM,
        scratch_shapes=[
            pltpu.VMEM((count, near, height, rank), f32),
            dma((count,)),
            dma((count,)),
            dma((2, max(groups - 1, 1))),
            dma((2, max(groups - 1, 1))),
        ],
        compiler_params=pltpu.CompilerParams(collective_id=1, has_side_effects=True),
        name="gather_rows",
    )(part.reshape(near, rank, rank))
    flat = gathered.reshape(groups * blocks, wide)

    spots = jnp.arange(groups * blocks, dtype=jnp.int32)
    numbers = (spots // blocks) * (2 * local) + spots % blocks - 1
    slot_of = jnp.where(numbers >= 0, jnp.take(seq_slots, jnp.maximum(numbers, 0)), -1)
    chosen = (jnp.arange(seq_count, dtype=jnp.int32)[:, None] == slot_of[None, :]).astype(f32)
    all_grads = jnp.dot(chosen, flat, precision=highest)
    own = lax.dynamic_slice_in_dim(all_grads, tok * local, local, 0)
    other = lax.dynamic_slice_in_dim(all_grads, (tok + 1 - 2 * half) * local, local, 0)
    products = [
        lax.dot_general(rows_, all_grads, (((1,), (1,)), ((), ())), precision=highest)
        for rows_ in (kept, taken)
    ]
    is_low = half == 0
    low = jnp.where(is_low, products[0], products[1])
    high = jnp.where(is_low, products[1], products[0])
    pad = -seq_count % 128
    scores_part = jnp.pad(jnp.concatenate([low, high], axis=0), ((0, 0), (0, pad)))
    score_rows = store_rows // feats
    scores_part = scores_part.reshape(count, score_rows, seq_count + pad)
    traded, scores = pl.pallas_call(
        functools.partial(last_kernel, feats),
        out_shape=[
            jax.ShapeDtypeStruct((local, wide), f32),
            jax.ShapeDtypeStruct((score_rows, seq_count + pad), f32),
        ],
        in_specs=[VMEM] * 2,
        out_specs=[VMEM] * 2,
        scratch_shapes=[
            pltpu.VMEM((count, score_rows, seq_count + pad), f32),
            dma((count,)),
            dma((count,)),
            dma,
            dma,
        ],
        compiler_params=pltpu.CompilerParams(collective_id=2, has_side_effects=True),
        name="last_rows",
    )(other, scores_part)
    own_rows = jnp.concatenate(
        [jnp.where(is_low, own, traded), jnp.where(is_low, traded, own)], axis=1
    )
    return scores[:, :seq_count], own_rows


def solution(mesh):
    placed = (
        P("tok", "feat"),
        P("tok", "feat"),
        P("feat", None),
        P("feat", None),
        P(),
        P(),
        P(),
        P(),
        P("tok", "feat"),
    )
    return jax.shard_map(
        body,
        mesh=mesh,
        in_specs=placed,
        out_specs=(P(("tok", "feat"), None), P("tok", "feat")),
        check_vma=False,
    )
```

time: 195 us -> 133 us (0.68)
  waiting for transfers between devices: 130 us -> 0.01 us
  Pallas kernels: 0 us -> 86 us
  between operations: 14.9 us -> 0.82 us
  blocking collectives: 10.1 us -> 0 us
  matrix products: 23.5 us -> 28.4 us
    pallas_call x0 -> x3, Pallas kernels: none -> 86 us  [the longest x1 56.2 us: body(): pl.pallas_call(functools.partial(gather_kernel, feats, groups, local, hei...]
    all_gather x1 -> x0, waiting for transfers between devices: 71.6 us -> none  [body(): by_sequence = lax.all_gather(finished, 'tok', axis=0, tiled=True)]
    psum x1 -> x0, waiting for transfers between devices: 53.5 us -> none  [body(): in_total, out_total = lax.psum((in_part, out_part), 'feat')]
    unnamed x1 -> x0, blocking collectives: 10.1 us -> none
    gather x1, local copies, waits for them, and re-layouts: 7.64 us -> 1.23 us  [body(): jnp.take(seq_slots, jnp.maximum(numbers, 0))]
    dot_general x4 -> x6, matrix products: 19.3 us -> 25.4 us  [the longest x1 8.3 us: body(): in_part = jnp.dot(activations, proj_in, preferred_element_type=f32)]
    unnamed x21 -> x13, local copies, waits for them, and re-layouts: 2.09 us -> 7.47 us
    ppermute x1, waiting for transfers between devices: 4.49 us -> 0.01 us  [body(): lax.ppermute(given, 'tok', [(t, t + 1 - 2 * (t % 2)) for t in range(toks)])]
  transfers between devices with their start and end apart: 3 -> 1, of which waited for: 3 -> 0; matrix products, arithmetic and copies ran while one was open for 1% -> 26% of each run, Pallas kernels for 0% -> 56%
where the time goes in v1:
time: 133 us
  Pallas kernels  86 us (65%)
  matrix products  28.4 us (21%)
  local copies, waits for them, and re-layouts  10.4 us (8%)
  other arithmetic  4.38 us (3%)
  starting transfers between devices  3.03 us (2%)
    pallas_call x1, Pallas kernels, body(): pl.pallas_call(functools.partial(gather_kernel, feats, groups, local, hei...  56.2 us
    pallas_call x1, Pallas kernels, body(): pl.pallas_call(functools.partial(sum_kernel, chips, rows), out_shape=[jax...  18.2 us
    pallas_call x1, Pallas kernels, body(): pl.pallas_call(functools.partial(last_kernel, feats), out_shape=[jax.Shap...  11.6 us
    dot_general x1, matrix products, body(): in_part = jnp.dot(activations, proj_in, preferred_element_type=f32)  8.3 us
    unnamed x13, local copies, waits for them, and re-layouts  7.47 us
    dot_general x2, matrix products, body(): lax.dot_general(rows_, all_grads, (((1,), (1,)), ((), ())), precision=hig...  6.5 us
    dot_general x1, matrix products, body(): out_part = jnp.dot(out_grads, proj_out, preferred_element_type=f32)  4.86 us
    dot_general x1, matrix products, body(): all_grads = jnp.dot(chosen, flat, precision=highest)  4.26 us
  transfers between devices with their start and end apart: 1, of which 0 were waited for; matrix products, arithmetic and copies ran while one was open for 26% of the time, Pallas kernels for 56%

profile of v1, /device:TPU:0, one launch (start us, length us, event | category | flops | bytes accessed | tf_op | source)
XLA Modules:
  0.0 133.0 jit_solution(3954157445489345828)
XLA Ops:
  0.7 1.6 %copy-done = f32[32,16384]{1,0:T(8,128)S(1)} copy-done((f32[32,16384]{1,0:T(8,128)S(1)}, f32[32,16384]{1,0:T(8,128)}, u32[]{:S(2)}) %copy-start) | copy-done | bytes 2097176
  2.3 3.0 %collective-permute-start = (f32[32,8192]{1,0:T(8,128)S(1)}, f32[32,8192]{1,0:T(8,128)}, u32[]{:S(2)}, u32[]{:S(2)}) collective-permute-start(f32[32,8192]{1,0:T(8,128)S(1)} %constant_dynamic-slice_fusion), channel_id=1, source_target_pairs={{0,4},{4,0},{8,12},{12,8},{16,20},{20,16},{24,28},{28,24},{1,5},{5... | collective-permute-start | bytes 3145736 | tf_op jit(solution)/shard_map/ppermute | solution.py:198
  5.4 0.7 copy.12
  6.3 0.7 sub.35
  7.1 0.7 pad_add_fusion.1
  8.1 4.9 %fusion.22.refs_0_ = f32[1024,256]{1,0:T(8,128)} fusion(bf16[1024,2048]{1,0:T(8,128)(2,1)} %param.10, bf16[2048,256]{1,0:T(8,128)(2,1)} %param.12), kind=kOutput, calls=%fused_computation.55 | convolution fusion | flops 1073741824 | bytes 6291456 | tf_op jit(solution)/shard_map/dot_general | solution.py:200
  13.0 8.3 %fusion.23.refs_1_ = f32[1024,256]{1,0:T(8,128)} fusion(bf16[1024,7168]{1,0:T(8,128)(2,1)} %param.9, bf16[7168,256]{1,0:T(8,128)(2,1)S(1)} %copy-done.4), kind=kOutput, calls=%fused_computation.56 | convolution fusion | flops 3758096384 | bytes 19398656 | tf_op jit(solution)/shard_map/dot_general | solution.py:201
  21.3 18.2 %sum_rows.1 = (f32[256,256]{1,0:T(8,128)}, f32[256,256]{1,0:T(8,128)}) custom-call(f32[1024,256]{1,0:T(8,128)} %fusion.22.refs_0_, f32[1024,256]{1,0:T(8,128)} %fusion.23.refs_1_), custom_call_target="tpu_custom_call" | custom-call | tf_op jit(solution)/shard_map/sum_rows/pallas_call | solution.py:202
  39.5 1.3 fusion.24
  40.8 1.4 %broadcast_multiply_fusion.2 = (f32[256,256]{0,1:T(8,128)S(1)}, f32[256,256]{0,1:T(8,128)S(1)}, f32[256,256]{0,1:T(8,128)S(1)}) fusion(f32[256]{0:T(256)S(1)} %bitcast.32, f32[256]{0:T(256)S(1)} %bitcast.33, f32[256]{0:T(256)S(1)} %bitcast.34, f32[256,256]{1,0:T(8,128)} %get-tuple-element.6, f32[256,256]{1,0:T(8,128)} %param.13), kind=kOutput, calls=%fused_computation.14 | convolution fusion | flops 201523200 | bytes 1313792 | tf_op jit(solution)/shard_map/dot_general | solution.py:212
  42.3 1.7 %fusion.2 = f32[768,256]{1,0:T(8,128)} fusion(f32[256,256]{1,0:T(8,128)S(1)} %fusion.24, f32[256,256]{0,1:T(8,128)S(1)} %get-tuple-element.13, f32[256,256]{0,1:T(8,128)S(1)} %get-tuple-element.14, f32[256,256]{0,1:T(8,128)S(1)} %get-tuple-element.12), kind=kOutput, calls=%fused_computation.3 | convolution fusion | flops 604372992 | bytes 1835008 | tf_op jit(solution)/shard_map/dot_general | solution.py:227
  44.0 56.2 %gather_rows.1 = f32[4,17,32,256]{3,2,1,0:T(8,128)} custom-call(f32[3,256,256]{2,1,0:T(8,128)} %bitcast.30), custom_call_target="tpu_custom_call" | custom-call | tf_op jit(solution)/shard_map/gather_rows/pallas_call | solution.py:230
  100.2 1.8 %pad.21 = f32[72,32,256]{2,1,0:T(8,128)S(1)} pad(f32[68,32,256]{2,1,0:T(8,128)} %bitcast.29, f32[]{:T(128)} %constant.99.clone.1), padding=0_4x0_0x0_0 | pad | bytes 4587524
  102.0 2.8 %copy.13 = f32[9,8,32,256]{3,1,2,0:T(8,128)} copy(f32[9,8,32,256]{3,2,1,0:T(8,128)S(1)} %bitcast.28) | data formatting | bytes 4718592
  104.8 1.2 gather_fusion
  106.1 4.3 %fusion.9 = f32[64,8192]{1,0:T(8,128)} fusion(f32[68,8192]{1,0:T(8,128)} %bitcast.27, s32[68]{0:T(128)S(1)} %compare_select_fusion.1), kind=kOutput, calls=%fused_computation.19 | convolution fusion | flops 427823360 | bytes 4325648 | tf_op jit(solution)/shard_map/dot_general | solution.py:251
  110.3 3.5 %fusion = f32[32,64]{1,0:T(8,128)S(1)} fusion(f32[64,8192]{1,0:T(8,128)} %fusion.9, f32[32,16384]{1,0:T(8,128)S(1)} %copy-done, s32[]{:T(128)S(6)} %select_n.128), kind=kOutput, calls=%fused_computation.1 | convolution fusion | flops 201326592 | bytes 3153924 | tf_op jit(solution)/shard_map/dot_general | solution.py:255
  113.8 0.7 constant_dynamic-slice_fusion.1.rows
  114.6 3.0 %broadcast_select_fusion.1 = (f32[32,64]{1,0:T(8,128)S(1)}, f32[32,64]{1,0:T(8,128)S(1)}) fusion(f32[32,64]{1,0:T(8,128)S(1)} %fusion, pred[]{:T(512)S(6)} %eq.23, f32[32,8192]{1,0:T(8,128)} %collective-permute-done, f32[64,8192]{1,0:T(8,128)S(1)} %copy-done.2), kind=kOutput, calls=%fused_computation.22 | convolution fusion | flops 201330688 | bytes 3170305 | tf_op jit(solution)/shard_map/dot_general | solution.py:255
  117.6 0.6 fusion.8.scores
  118.2 11.6 %last_rows.1 = (f32[8,8192]{1,0:T(8,128)}, f32[8,128]{1,0:T(8,128)}) custom-call(f32[8,8192]{1,0:T(8,128)} %constant_dynamic-slice_fusion.1.rows, f32[8,8,128]{2,1,0:T(8,128)} %fusion.8.scores), custom_call_target="tpu_custom_call" | custom-call | tf_op jit(solution)/shard_map/last_rows/pallas_call | solution.py:265
  129.8 1.1 dynamic-slice_select_fusion.1
  130.9 0.8 pad_maximum_fusion
  131.7 1.3 copy.15
  (23 shorter events, 0.7 us)
Async XLA Ops:
  0.6 1.6 %copy-start = (f32[32,16384]{1,0:T(8,128)S(1)}, f32[32,16384]{1,0:T(8,128)}, u32[]{:S(2)}) copy-start(f32[32,16384]{1,0:T(8,128)} %param.17) | copy-start | bytes 6291460
  2.3 112.3 %collective-permute-start = (f32[32,8192]{1,0:T(8,128)S(1)}, f32[32,8192]{1,0:T(8,128)}, u32[]{:S(2)}, u32[]{:S(2)}) collective-permute-start(f32[32,8192]{1,0:T(8,128)S(1)} %constant_dynamic-slice_fusion), channel_id=1, source_target_pairs={{0,4},{4,0},{8,12},{12,8},{16,20},{20,16},{24,28},{28,24},{1,5},{5... | collective-permute-start | bytes 3145736 | tf_op jit(solution)/shard_map/ppermute | solution.py:198
  8.1 4.9 %copy-start.4 = (bf16[7168,256]{1,0:T(8,128)(2,1)S(1)}, bf16[7168,256]{1,0:T(8,128)(2,1)}, u32[]{:S(2)}) copy-start(bf16[7168,256]{1,0:T(8,128)(2,1)} %param.11) | copy-start | bytes 11010052
  13.0 26.5 %copy-start.3 = (f32[256,256]{1,0:T(8,128)S(1)}, f32[256,256]{1,0:T(8,128)}, u32[]{:S(2)}) copy-start(f32[256,256]{1,0:T(8,128)} %param.14) | copy-start | bytes 786436
  102.0 2.8 %copy-start.1 = (s32[64]{0:T(128)S(1)}, s32[64]{0:T(128)}, u32[]{:S(2)}) copy-start(s32[64]{0:T(128)} %param.16) | copy-start | bytes 772
  110.3 3.5 %copy-start.2 = (f32[64,8192]{1,0:T(8,128)S(1)}, f32[64,8192]{1,0:T(8,128)}, u32[]{:S(2)}) copy-start(f32[64,8192]{1,0:T(8,128)} %fusion.9) | copy-start | bytes 6291460

commit v2 on v1

v2 whole, which is shorter than its diff:
```python
import functools

import jax
import jax.numpy as jnp
from jax import lax
from jax.experimental import pallas as pl
from jax.experimental.pallas import tpu as pltpu
from jax.sharding import PartitionSpec as P

MESH = pl.DeviceIdType.MESH
VMEM = pl.BlockSpec(memory_space=pltpu.VMEM)


def remote(src, dst, send_sem, recv_sem, tok, feat):
    return pltpu.make_async_remote_copy(
        src_ref=src, dst_ref=dst, send_sem=send_sem, recv_sem=recv_sem,
        device_id=(tok, feat), device_id_type=MESH,
    )


def greet(barrier, tok, feat):
    pl.semaphore_signal(barrier, inc=1, device_id=(tok, feat), device_id_type=MESH)


def sum_kernel(chips, rows, *refs):
    ins, outs, first, held, second = refs[0:2], refs[2:4], refs[4:6], refs[6:8], refs[8:10]
    send1, recv1, send2, recv2 = refs[10:14]
    tok, feat = lax.axis_index("tok"), lax.axis_index("feat")
    pair, core = feat // 2, feat % 2
    mate = pair * 2 + (1 - core)
    barrier = pltpu.get_barrier_semaphore()
    greet(barrier, tok, mate)
    for step in range(1, chips):
        greet(barrier, tok, ((pair + step) % chips) * 2 + core)
    pl.semaphore_wait(barrier, chips)

    def block(ref, step, side):
        owner = ((pair + step) % chips) * 2 + side
        return ref.at[pl.ds(pl.multiple_of(owner * rows, rows), rows)]

    order = [(step, k) for step in list(range(1, chips)) + [0] for k in range(2)]
    copies1 = {}
    for step, k in order:
        copies1[step, k] = remote(
            block(ins[k], step, 1 - core), first[k].at[step],
            send1.at[k, step], recv1.at[k, step], tok, mate,
        )
        copies1[step, k].start()
    copies2 = {}
    for step, k in order:
        copies1[step, k].wait_recv()
        held[k][step] = block(ins[k], step, core)[...] + first[k][step]
        if step:
            copies2[step, k] = remote(
                held[k].at[step], second[k].at[step],
                send2.at[k, step], recv2.at[k, step], tok, ((pair + step) % chips) * 2 + core,
            )
            copies2[step, k].start()
    for k in range(2):
        total = held[k][0]
        for step in range(1, chips):
            copies2[step, k].wait_recv()
            total += second[k][step]
        outs[k][...] = total
    for copy in list(copies1.values()) + list(copies2.values()):
        copy.wait_send()


def grads_kernel(sizes, part, chosen, *refs):
    feats, group_toks, groups, local, rows, spacing, pieces = sizes
    stored = refs[:group_toks]
    total, out = refs[group_toks : group_toks + 2]
    recv, grads, heads, picked, scored, landed = refs[group_toks + 2 : group_toks + 8]
    sends, recvs, gsend, grecv, hsend, hrecv, psend, precv, ssend, srecv = refs[group_toks + 8 :]
    highest = lax.Precision.HIGHEST
    near, count, height, rank = part.shape
    held = group_toks * local
    tall = height // pieces
    tok, feat = lax.axis_index("tok"), lax.axis_index("feat")
    group, spot = tok // group_toks, tok % group_toks
    me = spot * feats + feat

    def place(step):
        peer = (me + step) % count
        return peer // feats, peer % feats

    barrier = pltpu.get_barrier_semaphore()
    for step in range(1, count):
        peer_spot, peer_feat = place(step)
        greet(barrier, group * group_toks + peer_spot, peer_feat)

    @pl.when(group > 0)
    def _():
        greet(barrier, tok - group_toks, feat)

    @pl.when(group < groups - 1)
    def _():
        greet(barrier, tok + group_toks, feat)

    ends = (group > 0).astype(jnp.int32) + (group < groups - 1).astype(jnp.int32)
    pl.semaphore_wait(barrier, count - 1 + ends)

    copies = {}
    for piece in range(pieces):
        lines = pl.ds(piece * tall, tall)
        for step in range(1, count):
            peer_spot, peer_feat = place(step)
            copies[piece, step] = remote(
                part.at[:, peer_feat * group_toks + peer_spot, lines, :],
                recv.at[step, :, lines, :],
                sends.at[piece, step], recvs.at[piece, step],
                group * group_toks + peer_spot, peer_feat,
            )
            copies[piece, step].start()
    recv[0] = part[:, feat * group_toks + spot]

    terms = {}
    for source in range(count):
        base = (source // feats) * local + ((source % feats) * rows) // spacing
        for k in range(near):
            terms.setdefault(base + k, []).append((source, k))

    def block(at, piece):
        return grads.at[
            pl.ds(piece * tall, tall), pl.ds(pl.multiple_of(at * held, held), held), :
        ]

    def move(way, step, piece):
        at = jnp.clip(group - step if way == 0 else group + step, 0, groups - 1)
        to = tok + group_toks if way == 0 else tok - group_toks
        head = heads.at[at, pl.ds(piece * tall, tall), :]
        index = way, step, piece
        return (
            remote(block(at, piece), block(at, piece), gsend.at[index], grecv.at[index], to, feat),
            remote(head, head, hsend.at[index], hrecv.at[index], to, feat),
        )

    def each(way, step, piece, what, when):
        @pl.when(when)
        def _():
            for copy in move(way, step, piece):
                getattr(copy, what)()

    def sending(way, step):
        if way == 0:
            return (group - step >= 0) & (group + 1 < groups)
        return (group + step < groups) & (group - 1 >= 0)

    def taking(way, step):
        return group - 1 - step >= 0 if way == 0 else group + 1 + step < groups

    for piece in range(pieces):
        lines = pl.ds(piece * tall, tall)
        for step in range(1, count):
            copies[piece, step].wait_recv()
        for row in range(held + 1):
            value = None
            for source, k in terms.get(row, []):
                term = recv[(me + count - source) % count, k, lines, :]
                value = term if value is None else value + term
            if row == 0:
                heads[group, lines, :] = value
            else:
                block(group, piece)[:, row - 1, :] = value
        for way in range(2):
            if groups > 1:
                each(way, 0, piece, "start", sending(way, 0))
    for step in range(groups - 1):
        for piece in range(pieces):
            for way in range(2):
                each(way, step, piece, "wait_recv", taking(way, step))
                if step + 1 < groups - 1:
                    each(way, step + 1, piece, "start", sending(way, step + 1))
    for step in range(groups - 1):
        for piece in range(pieces):
            for way in range(2):
                each(way, step, piece, "wait_send", sending(way, step))

    for at in range(1, groups):
        grads[:, at * held - 1, :] += heads[at]
    pick = chosen[...]
    for line in range(height):
        lane = pl.ds(line * rank, rank)
        taken = jnp.dot(pick, grads[line], precision=highest, preferred_element_type=jnp.float32)
        for q in range(group_toks):
            picked[q, :, lane] = taken[q * local : (q + 1) * local]
    wide = height * rank
    mine = pl.ds(pl.multiple_of(spot * wide, wide), wide)
    trades = []
    for step in range(1, group_toks):
        to = (spot + step) % group_toks
        trades.append(remote(
            picked.at[to], out.at[:, mine], psend.at[step], precv.at[step],
            group * group_toks + to, feat,
        ))
        trades[-1].start()
    out[:, mine] = picked[spot]

    score = jnp.zeros((group_toks * stored[0].shape[0], grads.shape[1]), jnp.float32)
    for line in range(height):
        lane = pl.ds(line * rank, rank)
        kept = jnp.concatenate([ref[:, lane] for ref in stored], axis=0)
        score += lax.dot_general(
            kept, grads[line], (((1,), (1,)), ((), ())),
            precision=highest, preferred_element_type=jnp.float32,
        )
    scored[...] = jnp.zeros_like(scored)
    few = total.shape[0]
    for step in range(group_toks):
        for f in range(feats):
            first = (step * feats + f) * few
            scored[step, f, :, : score.shape[1]] = score[first : first + few]
    parts = []
    for step in range(group_toks):
        for turn in range(feats):
            if step or turn:
                to = (feat + turn) % feats
                parts.append(remote(
                    scored.at[step, to], landed.at[step, turn],
                    ssend.at[step, turn], srecv.at[step, turn],
                    group * group_toks + (spot + group_toks - step) % group_toks, to,
                ))
                parts[-1].start()
    summed = scored[0, feat]
    for number, copy in enumerate(parts, 1):
        copy.wait_recv()
        summed += landed[number // feats, number % feats]
    total[...] = summed
    for copy in trades:
        copy.wait_recv()
    for copy in trades + parts + list(copies.values()):
        copy.wait_send()


def body(
    activations,
    out_grads,
    proj_in,
    proj_out,
    left_factor,
    right_factor,
    seq_lengths,
    seq_slots,
    stored_grads,
):
    highest = lax.Precision.HIGHEST
    f32 = jnp.float32
    dma = pltpu.SemaphoreType.DMA
    feats, toks = lax.axis_size("feat"), lax.axis_size("tok")
    group_toks = 4 if toks % 4 == 0 else 1
    chips, groups, count = feats // 2, toks // group_toks, group_toks * feats
    rank = right_factor.shape[0]
    tok_rows = activations.shape[0]
    seq_count = seq_lengths.shape[0]
    local = seq_count // toks
    spacing = tok_rows // local
    rows = tok_rows // feats
    height = rank // count
    near = max(rows // spacing, 1) + 1
    feat, tok = lax.axis_index("feat"), lax.axis_index("tok")
    spot = tok % group_toks
    store_rows, width = stored_grads.shape
    wide = width // group_toks

    stored = []
    for step in range(group_toks):
        to = (spot + step) % group_toks
        given = lax.dynamic_slice_in_dim(stored_grads, to * wide, wide, 1)
        pairs = [(t, t - t % group_toks + (t + step) % group_toks) for t in range(toks)]
        stored.append(lax.ppermute(given, "tok", pairs) if step else given)

    out_part = jnp.dot(out_grads, proj_out, preferred_element_type=f32)
    in_part = jnp.dot(activations, proj_in, preferred_element_type=f32)
    out_total, in_total = pl.pallas_call(
        functools.partial(sum_kernel, chips, rows),
        out_shape=[jax.ShapeDtypeStruct((rows, rank), f32)] * 2,
        in_specs=[VMEM] * 2,
        out_specs=[VMEM] * 2,
        scratch_shapes=[pltpu.VMEM((chips, rows, rank), f32)] * 6 + [dma((2, chips))] * 4,
        compiler_params=pltpu.CompilerParams(collective_id=0, has_side_effects=True),
        name="sum_rows",
    )(out_part, in_part)
    right_side = jnp.dot(in_total, right_factor, precision=highest)
    left_side = jnp.dot(out_total, left_factor.T, precision=highest)

    places = tok * tok_rows + feat * rows + jnp.arange(rows, dtype=jnp.int32)
    numbers = jnp.arange(seq_count, dtype=jnp.int32)
    close = tok * local + (feat * rows) // spacing - 1 + jnp.arange(near, dtype=jnp.int32)
    starts = jnp.sum(jnp.where(numbers[None, :] < close[:, None], seq_lengths[None, :], 0), axis=1)
    sizes = jnp.sum(jnp.where(numbers[None, :] == close[:, None], seq_lengths[None, :], 0), axis=1)
    inside = (places[:, None] >= starts[None, :]) & (places[:, None] < (starts + sizes)[None, :])
    weights = inside.astype(f32) / jnp.maximum(sizes, 1).astype(f32)[None, :]
    spread = jnp.concatenate([weights[:, k : k + 1] * left_side for k in range(near)], axis=1)
    part = lax.dot_general(spread, right_side, (((0,), (0,)), ((), ())), precision=highest)

    held = group_toks * local
    slots = (tok // group_toks) * held + jnp.arange(held, dtype=jnp.int32)
    chosen = (slots[:, None] == seq_slots[None, :]).astype(f32)
    score_rows = store_rows // feats
    lanes = seq_count + -seq_count % 128
    pieces = 2 if height % 16 == 0 else 1
    hops = max(groups - 1, 1)
    sizes_ = (feats, group_toks, groups, local, rows, spacing, pieces)
    scores, own_rows = pl.pallas_call(
        functools.partial(grads_kernel, sizes_),
        out_shape=[
            jax.ShapeDtypeStruct((score_rows, lanes), f32),
            jax.ShapeDtypeStruct((local, width), f32),
        ],
        in_specs=[VMEM] * (2 + group_toks),
        out_specs=[VMEM] * 2,
        scratch_shapes=[
            pltpu.VMEM((count, near, height, rank), f32),
            pltpu.VMEM((height, seq_count, rank), f32),
            pltpu.VMEM((groups, height, rank), f32),
            pltpu.VMEM((group_toks, local, wide), f32),
            pltpu.VMEM((group_toks, feats, score_rows, lanes), f32),
            pltpu.VMEM((group_toks, feats, score_rows, lanes), f32),
        ]
        + [dma((pieces, count))] * 2
        + [dma((2, hops, pieces))] * 4
        + [dma((group_toks,))] * 2
        + [dma((group_toks, feats))] * 2,
        compiler_params=pltpu.CompilerParams(collective_id=1, has_side_effects=True),
        name="grads",
    )(part.reshape(near, count, height, rank), chosen, *stored)
    slot_of = (seq_slots[:, None] == numbers[None, :]).astype(f32)
    return jnp.dot(scores[:, :seq_count], slot_of, precision=highest), own_rows


def solution(mesh):
    placed = (
        P("tok", "feat"),
        P("tok", "feat"),
        P("feat", None),
        P("feat", None),
        P(),
        P(),
        P(),
        P(),
        P("tok", "feat"),
    )
    return jax.shard_map(
        body,
        mesh=mesh,
        in_specs=placed,
        out_specs=(P(("tok", "feat"), None), P("tok", "feat")),
        check_vma=False,
    )
```

time: 133 us -> 99.1 us (0.75)
  Pallas kernels: 86 us -> 66.3 us
  matrix products: 28.4 us -> 19.5 us
  local copies, waits for them, and re-layouts: 10.4 us -> 5.72 us
  other arithmetic: 4.38 us -> 0.95 us
  starting transfers between devices: 3.03 us -> 5.08 us
    pallas_call x2 -> x1, Pallas kernels: 67.8 us -> 48.1 us  [body(): pl.pallas_call(functools.partial(grads_kernel, sizes_), out_shape=[jax.Sh...]
    dot_general x3 -> x1, matrix products: 10.8 us -> 1.47 us  [body(): jnp.dot(scores[:, :seq_count], slot_of, precision=highest)]
    unnamed x13 -> x17, local copies, waits for them, and re-layouts: 7.47 us -> 2.99 us
    dot_general x1, matrix products: 8.3 us -> 11.3 us  [body(): in_part = jnp.dot(activations, proj_in, preferred_element_type=f32)]
    dot_general x1, matrix products: 4.86 us -> 2.22 us  [body(): out_part = jnp.dot(out_grads, proj_out, preferred_element_type=f32)]
    ppermute x1 -> x3, starting transfers between devices: 3.03 us -> 5.08 us  [body(): stored.append(lax.ppermute(given, 'tok', pairs) if step else given)]
    dynamic_slice x4 -> x1, local copies, waits for them, and re-layouts: 0.94 us -> 2.72 us  [body(): given = lax.dynamic_slice_in_dim(stored_grads, to * wide, wide, 1)]
    concatenate x3 -> x0, other arithmetic: 1.63 us -> none  [the longest x1 0.83 us: body(): jnp.concatenate([jnp.where(is_low, own, traded), jnp.where(is_low, traded...]
  transfers between devices with their start and end apart: 1 -> 3, of which waited for: 0 -> 0; matrix products, arithmetic and copies ran while one was open for 26% -> 19% of each run, Pallas kernels for 56% -> 19%
where the time goes in v2:
time: 99.1 us; the launch traced here: 98.3 us
  Pallas kernels  66.3 us (67%)
  matrix products  19.5 us (20%)
  local copies, waits for them, and re-layouts  5.72 us (6%)
  starting transfers between devices  5.08 us (5%)
    pallas_call x1, Pallas kernels, body(): pl.pallas_call(functools.partial(grads_kernel, sizes_), out_shape=[jax.Sh...  48.1 us
    pallas_call x1, Pallas kernels, body(): pl.pallas_call(functools.partial(sum_kernel, chips, rows), out_shape=[jax...  18.2 us
    dot_general x1, matrix products, body(): in_part = jnp.dot(activations, proj_in, preferred_element_type=f32)  11.3 us
    ppermute x3, starting transfers between devices, body(): stored.append(lax.ppermute(given, 'tok', pairs) if step else given)  5.08 us
    unnamed x17, local copies, waits for them, and re-layouts  2.99 us
    dynamic_slice x1, local copies, waits for them, and re-layouts, body(): given = lax.dynamic_slice_in_dim(stored_grads, to * wide, wide, 1)  2.72 us
    dot_general x1, matrix products, body(): out_part = jnp.dot(out_grads, proj_out, preferred_element_type=f32)  2.22 us
  transfers between devices with their start and end apart: 3, of which 0 were waited for; matrix products, arithmetic and copies ran while one was open for 19% of the time, Pallas kernels for 19%

profile of v2, /device:TPU:0, one launch (start us, length us, event | category | flops | bytes accessed | tf_op | source)
XLA Modules:
  0.0 98.3 jit_solution(5859509014996017957)
XLA Ops:
  0.6 0.0 copy-start
  0.8 2.7 %constant_dynamic-slice_fusion.3 = (f32[32,4096]{1,0:T(8,128)}, f32[32,4096]{1,0:T(8,128)}, f32[32,4096]{1,0:T(8,128)}, f32[32,4096]{1,0:T(8,128)S(1)}) fusion(f32[32,16384]{1,0:T(8,128)} %param.17, s32[]{:T(128)S(6)} %select_n.61, s32[]{:T(128)S(6)} %select_n.57, s32[]{:T(128)S(6)} %select_n.55, s32[]{:T(128)S(6)} %select_n.59), kind=kLoop, calls=%fused_computation.22 | loop fusion | bytes 4194320 | tf_op jit(solution)/shard_map/dynamic_slice | solution.py:268
  3.5 4.0 %collective-permute-start.2 = (f32[32,4096]{1,0:T(8,128)}, f32[32,4096]{1,0:T(8,128)S(1)}, u32[]{:S(2)}, u32[]{:S(2)}) collective-permute-start(f32[32,4096]{1,0:T(8,128)} %get-tuple-element.12), channel_id=1, source_target_pairs={{0,12},{4,0},{8,4},{12,8},{16,28},{20,16},{24,20},{28,24},{1,13},{... | collective-permute-start | bytes 1572872 | tf_op jit(solution)/shard_map/ppermute | solution.py:270
  7.5 0.0 collective-permute-start
  7.5 1.1 %collective-permute-start.1 = (f32[32,4096]{1,0:T(8,128)S(1)}, f32[32,4096]{1,0:T(8,128)S(1)}, u32[]{:S(2)}, u32[]{:S(2)}) collective-permute-start(f32[32,4096]{1,0:T(8,128)S(1)} %get-tuple-element.15), channel_id=1, source_target_pairs={{0,8},{4,12},{8,0},{12,4},{16,24},{20,28},{24,16},{28,20},{1,9},{5... | collective-permute-start | bytes 1572872 | tf_op jit(solution)/shard_map/ppermute | solution.py:270
  8.6 0.2 select_reduce_fusion.1
  8.8 0.7 compare_convert_fusion.chosen
  9.4 11.3 %fusion.13.refs_1_ = f32[1024,256]{1,0:T(8,128)} fusion(bf16[1024,7168]{1,0:T(8,128)(2,1)} %param.9, bf16[7168,256]{1,0:T(8,128)(2,1)} %param.11), kind=kOutput, calls=%fused_computation.31 | convolution fusion | flops 3758096384 | bytes 19398656 | tf_op jit(solution)/shard_map/dot_general | solution.py:273
  20.8 2.2 %fusion.12.refs_0_ = f32[1024,256]{1,0:T(8,128)} fusion(bf16[1024,2048]{1,0:T(8,128)(2,1)S(1)} %copy-done.7, bf16[2048,256]{1,0:T(8,128)(2,1)S(1)} %copy-done), kind=kOutput, calls=%fused_computation.30 | convolution fusion | flops 1073741824 | bytes 6291456 | tf_op jit(solution)/shard_map/dot_general | solution.py:272
  23.0 18.2 %sum_rows.1 = (f32[256,256]{1,0:T(8,128)}, f32[256,256]{1,0:T(8,128)}) custom-call(f32[1024,256]{1,0:T(8,128)} %fusion.12.refs_0_, f32[1024,256]{1,0:T(8,128)} %fusion.13.refs_1_), custom_call_target="tpu_custom_call" | custom-call | tf_op jit(solution)/shard_map/sum_rows/pallas_call | solution.py:274
  41.2 1.3 %fusion.14 = f32[256,256]{1,0:T(8,128)S(1)} fusion(f32[256,256]{1,0:T(8,128)} %get-tuple-element.7, f32[256,256]{1,0:T(8,128)S(1)} %copy-done.4), kind=kOutput, calls=%fused_computation.32 | convolution fusion | flops 201326592 | bytes 786432 | tf_op jit(solution)/shard_map/dot_general | solution.py:283
  42.6 0.1 convert_divide_fusion
  42.7 1.4 %broadcast_multiply_fusion.2 = (f32[256,256]{0,1:T(8,128)S(1)}, f32[256,256]{0,1:T(8,128)S(1)}, f32[256,256]{0,1:T(8,128)S(1)}) fusion(f32[256]{0:T(256)S(1)} %bitcast.14, f32[256]{0:T(256)S(1)} %bitcast.15, f32[256]{0:T(256)S(1)} %bitcast.16, f32[256,256]{1,0:T(8,128)} %get-tuple-element.6, f32[256,256]{1,0:T(8,128)} %param.13), kind=kOutput, calls=%fused_computation.8 | convolution fusion | flops 201523200 | bytes 1313792 | tf_op jit(solution)/shard_map/dot_general | solution.py:284
  44.1 1.7 %fusion = f32[768,256]{1,0:T(8,128)} fusion(f32[256,256]{1,0:T(8,128)S(1)} %fusion.14, f32[256,256]{0,1:T(8,128)S(1)} %get-tuple-element.17, f32[256,256]{0,1:T(8,128)S(1)} %get-tuple-element.18, f32[256,256]{0,1:T(8,128)S(1)} %get-tuple-element.16), kind=kOutput, calls=%fused_computation | convolution fusion | flops 604372992 | bytes 1835008 | tf_op jit(solution)/shard_map/dot_general | solution.py:294
  45.8 0.0 collective-permute-done.2.refs_3_
  45.8 0.0 collective-permute-done.refs_1_
  45.8 0.0 copy-start.2
  45.8 0.0 collective-permute-done.1.refs_2_
  45.8 0.8 copy-done.1
  46.6 0.1 copy-done.2
  46.8 0.2 copy-done.3
  46.9 48.1 %grads.1 = (f32[8,128]{1,0:T(8,128)}, f32[8,16384]{1,0:T(8,128)}) custom-call(f32[3,16,16,256]{3,2,1,0:T(8,128)} %bitcast.13, f32[32,64]{1,0:T(8,128)} %compare_convert_fusion.chosen, f32[32,4096]{1,0:T(8,128)} %get-tuple-element.14.refs_0_, f32[32,4096]{1,0:T(8,128)} %copy-done.2, f32[32,4096]{1,0:T(8,128)} %copy-done.3, f32[32,4096]{1,0:T(8,128)} %copy-done.1), custom_call_target="tpu_custom_call" | custom-call | tf_op jit(solution)/shard_map/grads/pallas_call | solution.py:304
  95.0 1.5 %fusion.6 = f32[8,64]{1,0:T(8,128)} fusion(s32[64]{0:T(128)S(1)} %copy-done.5, f32[8,128]{1,0:T(8,128)} %get-tuple-element.8), kind=kOutput, calls=%fused_computation.10 | convolution fusion | flops 397312 | bytes 6400 | tf_op jit(solution)/shard_map/dot_general | solution.py:328
  96.5 1.9 %copy.12 = f32[8,16384]{1,0:T(8,128)} copy(f32[8,16384]{1,0:T(8,128)} %get-tuple-element.27) | data formatting | bytes 1048576
  (16 shorter events, 0.0 us)
Async XLA Ops:
  0.6 20.1 %copy-start = (bf16[2048,256]{1,0:T(8,128)(2,1)S(1)}, bf16[2048,256]{1,0:T(8,128)(2,1)}, u32[]{:S(2)}) copy-start(bf16[2048,256]{1,0:T(8,128)(2,1)} %param.12) | copy-start | bytes 3145732
  0.6 7.9 %copy-start.6 = (s32[64]{0:T(128)S(1)}, s32[64]{0:T(128)}, u32[]{:S(2)}) copy-start(s32[64]{0:T(128)} %param.15) | copy-start | bytes 772
  0.7 8.1 %copy-start.5 = (s32[64]{0:T(128)S(1)}, s32[64]{0:T(128)}, u32[]{:S(2)}) copy-start(s32[64]{0:T(128)} %param.16) | copy-start | bytes 772
  3.5 42.3 %collective-permute-start.2 = (f32[32,4096]{1,0:T(8,128)}, f32[32,4096]{1,0:T(8,128)S(1)}, u32[]{:S(2)}, u32[]{:S(2)}) collective-permute-start(f32[32,4096]{1,0:T(8,128)} %get-tuple-element.12), channel_id=1, source_target_pairs={{0,12},{4,0},{8,4},{12,8},{16,28},{20,16},{24,20},{28,24},{1,13},{... | collective-permute-start | bytes 1572872 | tf_op jit(solution)/shard_map/ppermute | solution.py:270
  7.5 38.3 %collective-permute-start = (f32[32,4096]{1,0:T(8,128)}, f32[32,4096]{1,0:T(8,128)S(1)}, u32[]{:S(2)}, u32[]{:S(2)}) collective-permute-start(f32[32,4096]{1,0:T(8,128)} %get-tuple-element.13), channel_id=1, source_target_pairs={{0,4},{4,8},{8,12},{12,0},{16,20},{20,24},{24,28},{28,16},{1,5},{5... | collective-permute-start | bytes 1572872 | tf_op jit(solution)/shard_map/ppermute | solution.py:270
  7.5 38.4 %collective-permute-start.1 = (f32[32,4096]{1,0:T(8,128)S(1)}, f32[32,4096]{1,0:T(8,128)S(1)}, u32[]{:S(2)}, u32[]{:S(2)}) collective-permute-start(f32[32,4096]{1,0:T(8,128)S(1)} %get-tuple-element.15), channel_id=1, source_target_pairs={{0,8},{4,12},{8,0},{12,4},{16,24},{20,28},{24,16},{28,20},{1,9},{5... | collective-permute-start | bytes 1572872 | tf_op jit(solution)/shard_map/ppermute | solution.py:270
  9.4 11.3 %copy-start.7 = (bf16[1024,2048]{1,0:T(8,128)(2,1)S(1)}, bf16[1024,2048]{1,0:T(8,128)(2,1)}, u32[]{:S(2)}) copy-start(bf16[1024,2048]{1,0:T(8,128)(2,1)} %param.10) | copy-start | bytes 12582916
  20.8 20.5 %copy-start.4 = (f32[256,256]{1,0:T(8,128)S(1)}, f32[256,256]{1,0:T(8,128)}, u32[]{:S(2)}) copy-start(f32[256,256]{1,0:T(8,128)} %param.14) | copy-start | bytes 786436
  45.8 0.8 copy-start.1
  45.8 1.0 copy-start.2
  45.8 1.1 %copy-start.3 = (f32[32,4096]{1,0:T(8,128)}, f32[32,4096]{1,0:T(8,128)S(1)}, u32[]{:S(2)}) copy-start(f32[32,4096]{1,0:T(8,128)S(1)} %collective-permute-done.1.refs_2_) | copy-start | bytes 1572868

commit v3 on v2

--- a/solution.py
+++ b/solution.py
@@ -22,56 +22,114 @@
     pl.semaphore_signal(barrier, inc=1, device_id=(tok, feat), device_id_type=MESH)
 
 
-def sum_kernel(chips, rows, *refs):
-    ins, outs, first, held, second = refs[0:2], refs[2:4], refs[4:6], refs[6:8], refs[8:10]
-    send1, recv1, send2, recv2 = refs[10:14]
+def project_kernel(sizes, *refs):
+    chips, rows, group_toks, early = sizes
+    rows_in, mats_in, stored = refs[0:2], refs[2:4], refs[4]
+    outs, traded = refs[5:7], refs[7 : 7 + early]
+    refs = refs[7 + early :]
+    lhs, rhs, parts, first, held, second = (refs[2 * n : 2 * n + 2] for n in range(6))
+    load, send1, recv1, send2, recv2, tsend, trecv = refs[12:]
     tok, feat = lax.axis_index("tok"), lax.axis_index("feat")
+    spot = tok % group_toks
     pair, core = feat // 2, feat % 2
     mate = pair * 2 + (1 - core)
+    both = 2 * rows
+    order = list(range(1, chips)) + [0]
+
+    def lines(step):
+        return pl.ds(pl.multiple_of(((pair + step) % chips) * both, both), both)
+
+    loads = {}
+    for step in order:
+        for k in range(2):
+            if step == order[0]:
+                loads[k] = pltpu.make_async_copy(mats_in[k], rhs[k], load.at[k, chips])
+                loads[k].start()
+            loads[k, step] = pltpu.make_async_copy(
+                rows_in[k].at[lines(step)], lhs[k].at[step], load.at[k, step]
+            )
+            loads[k, step].start()
+
     barrier = pltpu.get_barrier_semaphore()
     greet(barrier, tok, mate)
     for step in range(1, chips):
         greet(barrier, tok, ((pair + step) % chips) * 2 + core)
-    pl.semaphore_wait(barrier, chips)
-
-    def block(ref, step, side):
-        owner = ((pair + step) % chips) * 2 + side
-        return ref.at[pl.ds(pl.multiple_of(owner * rows, rows), rows)]
-
-    order = [(step, k) for step in list(range(1, chips)) + [0] for k in range(2)]
-    copies1 = {}
-    for step, k in order:
-        copies1[step, k] = remote(
-            block(ins[k], step, 1 - core), first[k].at[step],
-            send1.at[k, step], recv1.at[k, step], tok, mate,
+    for step in range(1, group_toks):
+        greet(barrier, tok - spot + (spot + step) % group_toks, feat)
+    pl.semaphore_wait(barrier, chips + group_toks - 1)
+
+    wide = traded[0].shape[1]
+    trades = []
+    for step in range(1, early + 1):
+        to = (spot + step) % group_toks
+        trades.append(remote(
+            stored.at[:, pl.ds(pl.multiple_of(to * wide, wide), wide)], traded[step - 1],
+            tsend.at[step - 1], trecv.at[step - 1], tok - spot + to, feat,
+        ))
+        trades[-1].start()
+
+    copies1, copies2 = {}, {}
+
+    def project(k, step, low, high):
+        return jnp.dot(
+            lhs[k][step, :, low:high], rhs[k][low:high, :], preferred_element_type=jnp.float32
         )
-        copies1[step, k].start()
-    copies2 = {}
-    for step, k in order:
-        copies1[step, k].wait_recv()
-        held[k][step] = block(ins[k], step, core)[...] + first[k][step]
+
+    def to_mate(k, step):
+        copies1[k, step] = remote(
+            parts[k].at[step, pl.ds(pl.multiple_of((1 - core) * rows, rows), rows)],
+            first[k].at[step], send1.at[k, step], recv1.at[k, step], tok, mate,
+        )
+        copies1[k, step].start()
+
+    def onward(k, step):
+        copies1[k, step].wait_recv()
+        own = parts[k][step, pl.ds(pl.multiple_of(core * rows, rows), rows), :]
+        held[k][step] = own + first[k][step]
         if step:
-            copies2[step, k] = remote(
-                held[k].at[step], second[k].at[step],
-                send2.at[k, step], recv2.at[k, step], tok, ((pair + step) % chips) * 2 + core,
+            copies2[k, step] = remote(
+                held[k].at[step], second[k].at[step], send2.at[k, step], recv2.at[k, step],
+                tok, ((pair + step) % chips) * 2 + core,
             )
-            copies2[step, k].start()
+            copies2[k, step].start()
+
+    waiting = []
+    for number, step in enumerate(order):
+        for k in range(2):
+            if number == 0:
+                loads[k].wait()
+            loads[k, step].wait()
+            depth = lhs[k].shape[2]
+            cut = depth // 2 if k else depth
+            parts[k][step] = project(k, step, 0, cut)
+            for item in waiting:
+                onward(*item)
+            waiting = []
+            if cut < depth:
+                parts[k][step] += project(k, step, cut, depth)
+            to_mate(k, step)
+            waiting = [(k, step)]
+    for item in waiting:
+        onward(*item)
     for k in range(2):
         total = held[k][0]
         for step in range(1, chips):
-            copies2[step, k].wait_recv()
+            copies2[k, step].wait_recv()
             total += second[k][step]
         outs[k][...] = total
-    for copy in list(copies1.values()) + list(copies2.values()):
+    for copy in trades:
+        copy.wait_recv()
+    for copy in trades + list(copies1.values()) + list(copies2.values()):
         copy.wait_send()
 
 
-def grads_kernel(sizes, part, chosen, *refs):
-    feats, group_toks, groups, local, rows, spacing, pieces = sizes
-    stored = refs[:group_toks]
-    total, out = refs[group_toks : group_toks + 2]
-    recv, grads, heads, picked, scored, landed = refs[group_toks + 2 : group_toks + 8]
-    sends, recvs, gsend, grecv, hsend, hrecv, psend, precv, ssend, srecv = refs[group_toks + 8 :]
+def grads_kernel(sizes, part, chosen, slot_of, stored_rows, *refs):
+    feats, group_toks, groups, local, rows, spacing, pieces, early = sizes
+    total, out = refs[early : early + 2]
+    recv, grads, heads, picked, scored, landed, late = refs[early + 2 : early + 9]
+    sends, recvs, gsend, grecv, hsend, hrecv, psend, precv, ssend, srecv, lsend, lrecv = refs[
+        early + 9 :
+    ]
     highest = lax.Precision.HIGHEST
     near, count, height, rank = part.shape
     held = group_toks * local
@@ -113,6 +171,23 @@
             )
             copies[piece, step].start()
     recv[0] = part[:, feat * group_toks + spot]
+    width = late.shape[2]
+    kept = pltpu.make_async_copy(
+        stored_rows.at[:, pl.ds(pl.multiple_of(spot * width, width), width)], late.at[0], lsend.at[0]
+    )
+    kept.start()
+    trades = []
+    for step in range(early + 1, group_toks):
+        to = (spot + step) % group_toks
+        trades.append(remote(
+            stored_rows.at[:, pl.ds(pl.multiple_of(to * width, width), width)],
+            late.at[step - early], lsend.at[step - early], lrecv.at[step - early],
+            group * group_toks + to, feat,
+        ))
+        trades[-1].start()
+    stored = [late.at[0], *refs[:early]] + [
+        late.at[step - early] for step in range(early + 1, group_toks)
+    ]
 
     terms = {}
     for source in range(count):
@@ -186,7 +261,6 @@
             picked[q, :, lane] = taken[q * local : (q + 1) * local]
     wide = height * rank
     mine = pl.ds(pl.multiple_of(spot * wide, wide), wide)
-    trades = []
     for step in range(1, group_toks):
         to = (spot + step) % group_toks
         trades.append(remote(
@@ -196,16 +270,19 @@
         trades[-1].start()
     out[:, mine] = picked[spot]
 
-    score = jnp.zeros((group_toks * stored[0].shape[0], grads.shape[1]), jnp.float32)
+    kept.wait()
+    for copy in trades[: group_toks - 1 - early]:
+        copy.wait_recv()
+    score = jnp.zeros((group_toks * late.shape[1], grads.shape[1]), jnp.float32)
     for line in range(height):
         lane = pl.ds(line * rank, rank)
-        kept = jnp.concatenate([ref[:, lane] for ref in stored], axis=0)
+        lanes = jnp.concatenate([ref[:, lane] for ref in stored], axis=0)
         score += lax.dot_general(
-            kept, grads[line], (((1,), (1,)), ((), ())),
+            lanes, grads[line], (((1,), (1,)), ((), ())),
             precision=highest, preferred_element_type=jnp.float32,
         )
     scored[...] = jnp.zeros_like(scored)
-    few = total.shape[0]
+    few = scored.shape[2]
     for step in range(group_toks):
         for f in range(feats):
             first = (step * feats + f) * few
@@ -225,8 +302,11 @@
     for number, copy in enumerate(parts, 1):
         copy.wait_recv()
         summed += landed[number // feats, number % feats]
-    total[...] = summed
-    for copy in trades:
+    total[...] = jnp.dot(
+        summed[:, : score.shape[1]], slot_of[...], precision=highest,
+        preferred_element_type=jnp.float32,
+    )
+    for copy in trades[group_toks - 1 - early :]:
         copy.wait_recv()
     for copy in trades + parts + list(copies.values()):
         copy.wait_send()
@@ -262,24 +342,28 @@
     store_rows, width = stored_grads.shape
     wide = width // group_toks
 
-    stored = []
-    for step in range(group_toks):
-        to = (spot + step) % group_toks
-        given = lax.dynamic_slice_in_dim(stored_grads, to * wide, wide, 1)
-        pairs = [(t, t - t % group_toks + (t + step) % group_toks) for t in range(toks)]
-        stored.append(lax.ppermute(given, "tok", pairs) if step else given)
-
-    out_part = jnp.dot(out_grads, proj_out, preferred_element_type=f32)
-    in_part = jnp.dot(activations, proj_in, preferred_element_type=f32)
-    out_total, in_total = pl.pallas_call(
-        functools.partial(sum_kernel, chips, rows),
-        out_shape=[jax.ShapeDtypeStruct((rows, rank), f32)] * 2,
-        in_specs=[VMEM] * 2,
-        out_specs=[VMEM] * 2,
-        scratch_shapes=[pltpu.VMEM((chips, rows, rank), f32)] * 6 + [dma((2, chips))] * 4,
-        compiler_params=pltpu.CompilerParams(collective_id=0, has_side_effects=True),
-        name="sum_rows",
-    )(out_part, in_part)
+    early = max(group_toks - 2, 1)
+    any_space = pl.BlockSpec(memory_space=pl.ANY)
+    lefts, mats = (out_grads, activations), (proj_out, proj_in)
+    pair_rows = pltpu.VMEM((chips, rows, rank), f32)
+    out_total, in_total, *traded = pl.pallas_call(
+        functools.partial(project_kernel, (chips, rows, group_toks, early)),
+        out_shape=[jax.ShapeDtypeStruct((rows, rank), f32)] * 2
+        + [jax.ShapeDtypeStruct((store_rows, wide), f32)] * early,
+        in_specs=[any_space] * 5,
+        out_specs=[VMEM] * (2 + early),
+        scratch_shapes=[pltpu.VMEM((chips, 2 * rows, m.shape[1]), m.dtype) for m in lefts]
+        + [pltpu.VMEM(m.shape, m.dtype) for m in mats]
+        + [pltpu.VMEM((chips, 2 * rows, rank), f32)] * 2
+        + [pair_rows] * 6
+        + [dma((2, chips + 1))]
+        + [dma((2, chips))] * 4
+        + [dma((early,))] * 2,
+        compiler_params=pltpu.CompilerParams(
+            collective_id=0, has_side_effects=True, vmem_limit_bytes=60 << 20
+        ),
+        name="project",
+    )(*lefts, *mats, stored_grads)
     right_side = jnp.dot(in_total, right_factor, precision=highest)
     left_side = jnp.dot(out_total, left_factor.T, precision=highest)
 
@@ -300,14 +384,15 @@
     lanes = seq_count + -seq_count % 128
     pieces = 2 if height % 16 == 0 else 1
     hops = max(groups - 1, 1)
-    sizes_ = (feats, group_toks, groups, local, rows, spacing, pieces)
+    sizes_ = (feats, group_toks, groups, local, rows, spacing, pieces, early)
+    slot_of = (seq_slots[:, None] == numbers[None, :]).astype(f32)
     scores, own_rows = pl.pallas_call(
         functools.partial(grads_kernel, sizes_),
         out_shape=[
-            jax.ShapeDtypeStruct((score_rows, lanes), f32),
+            jax.ShapeDtypeStruct((score_rows, seq_count), f32),
             jax.ShapeDtypeStruct((local, width), f32),
         ],
-        in_specs=[VMEM] * (2 + group_toks),
+        in_specs=[VMEM] * 3 + [any_space] + [VMEM] * early,
         out_specs=[VMEM] * 2,
         scratch_shapes=[
             pltpu.VMEM((count, near, height, rank), f32),
@@ -316,16 +401,17 @@
             pltpu.VMEM((group_toks, local, wide), f32),
             pltpu.VMEM((group_toks, feats, score_rows, lanes), f32),
             pltpu.VMEM((group_toks, feats, score_rows, lanes), f32),
+            pltpu.VMEM((group_toks - early, store_rows, wide), f32),
         ]
         + [dma((pieces, count))] * 2
         + [dma((2, hops, pieces))] * 4
         + [dma((group_toks,))] * 2
-        + [dma((group_toks, feats))] * 2,
+        + [dma((group_toks, feats))] * 2
+        + [dma((group_toks - early,))] * 2,
         compiler_params=pltpu.CompilerParams(collective_id=1, has_side_effects=True),
         name="grads",
-    )(part.reshape(near, count, height, rank), chosen, *stored)
-    slot_of = (seq_slots[:, None] == numbers[None, :]).astype(f32)
-    return jnp.dot(scores[:, :seq_count], slot_of, precision=highest), own_rows
+    )(part.reshape(near, count, height, rank), chosen, slot_of, stored_grads, *traded)
+    return scores, own_rows
 
 
 def solution(mesh):

time: 99.1 us -> 89.7 us (0.905)
  matrix products: 19.5 us -> 4.37 us
  Pallas kernels: 66.3 us -> 78.8 us
  starting transfers between devices: 5.08 us -> 0 us
  local copies, waits for them, and re-layouts: 5.72 us -> 3.17 us
  other arithmetic: 0.95 us -> 2.36 us
    dot_general x3 -> x0, matrix products: 15 us -> none  [the longest x1 11.3 us: body(): in_part = jnp.dot(activations, proj_in, preferred_element_type=f32)]
    pallas_call x1, Pallas kernels: 48.1 us -> 55.3 us  [body(): pl.pallas_call(functools.partial(grads_kernel, sizes_), out_shape=[jax.Sh...]
    pallas_call x1, Pallas kernels: 18.2 us -> 23.5 us  [body(): pl.pallas_call(functools.partial(project_kernel, (chips, rows, group_toks...]
    ppermute x3 -> x0, starting transfers between devices: 5.08 us -> none  [body(): stored.append(lax.ppermute(given, 'tok', pairs) if step else given)]
    dynamic_slice x1 -> x0, local copies, waits for them, and re-layouts: 2.72 us -> none  [body(): given = lax.dynamic_slice_in_dim(stored_grads, to * wide, wide, 1)]
    unnamed x17 -> x8, local copies, waits for them, and re-layouts: 2.99 us -> 3.16 us
  transfers between devices with their start and end apart: 3 -> 0, of which waited for: 0 -> 0; matrix products, arithmetic and copies ran while one was open for 19% -> 0% of each run, Pallas kernels for 19% -> 0%
where the time goes in v3:
time: 89.7 us; the launch traced here: 89.4 us
  Pallas kernels  78.8 us (88%)
  matrix products  4.37 us (5%)
  local copies, waits for them, and re-layouts  3.17 us (4%)
  other arithmetic  2.36 us (3%)
    pallas_call x1, Pallas kernels, body(): pl.pallas_call(functools.partial(grads_kernel, sizes_), out_shape=[jax.Sh...  55.3 us
    pallas_call x1, Pallas kernels, body(): pl.pallas_call(functools.partial(project_kernel, (chips, rows, group_toks...  23.5 us
    unnamed x8, local copies, waits for them, and re-layouts  3.16 us

profile of v3, /device:TPU:0, one launch (start us, length us, event | category | flops | bytes accessed | tf_op | source)
XLA Modules:
  0.0 89.4 jit_solution(10521210354154593964)
XLA Ops:
  0.6 0.0 copy-start
  0.7 0.9 %select_reduce_fusion.1 = (s32[3]{0:T(128)S(1)}, s32[3]{0:T(128)S(1)}) fusion(s32[64]{0:T(128)} %param.15, s32[3]{0:T(128)S(1)} %iota_add_fusion.2), kind=kLoop, calls=%fused_computation.15 | loop fusion | flops 1146 | bytes 292 | tf_op jit(solution)/shard_map/reduce_sum | solution.py:373
  1.6 0.1 convert_divide_fusion
  1.7 0.0 copy-start.1
  1.7 0.0 copy-start.2
  1.7 23.5 %project.1 = (f32[256,256]{1,0:T(8,128)}, f32[256,256]{1,0:T(8,128)}, f32[32,4096]{1,0:T(8,128)}, f32[32,4096]{1,0:T(8,128)}) custom-call(bf16[1024,2048]{1,0:T(8,128)(2,1)} %refs_0_.1, bf16[1024,7168]{1,0:T(8,128)(2,1)} %refs_1_.1, bf16[2048,256]{1,0:T(8,128)(2,1)} %refs_2_.1, bf16[7168,256]{1,0:T(8,128)(2,1)} %refs_3_.1, f32[32,16384]{1,0:T(8,128)} %stored_rows.1), custom_call_target="tpu_custom_call" | custom-call | tf_op jit(solution)/shard_map/project/pallas_call | solution.py:349
  25.2 0.0 copy-done
  25.2 1.4 %broadcast_multiply_fusion.2 = (f32[256,256]{0,1:T(8,128)S(1)}, f32[256,256]{0,1:T(8,128)S(1)}, f32[256,256]{0,1:T(8,128)S(1)}) fusion(f32[256]{0:T(256)S(1)} %bitcast.10, f32[256]{0:T(256)S(1)} %bitcast.11, f32[256]{0:T(256)S(1)} %bitcast.12, f32[256,256]{1,0:T(8,128)} %get-tuple-element.6, f32[256,256]{1,0:T(8,128)S(1)} %copy-done), kind=kOutput, calls=%fused_computation.8 | convolution fusion | flops 201523200 | bytes 1313792 | tf_op jit(solution)/shard_map/dot_general | solution.py:368
  26.6 0.0 copy-done.1
  26.6 1.3 %fusion.10 = f32[256,256]{1,0:T(8,128)S(1)} fusion(f32[256,256]{1,0:T(8,128)} %get-tuple-element.7, f32[256,256]{1,0:T(8,128)S(1)} %copy-done.1), kind=kOutput, calls=%fused_computation.24 | convolution fusion | flops 201326592 | bytes 786432 | tf_op jit(solution)/shard_map/dot_general | solution.py:367
  27.9 1.7 %fusion = f32[768,256]{1,0:T(8,128)} fusion(f32[256,256]{1,0:T(8,128)S(1)} %fusion.10, f32[256,256]{0,1:T(8,128)S(1)} %get-tuple-element.13, f32[256,256]{0,1:T(8,128)S(1)} %get-tuple-element.14, f32[256,256]{0,1:T(8,128)S(1)} %get-tuple-element.12), kind=kOutput, calls=%fused_computation | convolution fusion | flops 604372992 | bytes 1835008 | tf_op jit(solution)/shard_map/dot_general | solution.py:378
  29.6 0.0 copy-done.2
  29.6 0.7 compare_convert_fusion.chosen
  30.3 0.7 fusion.6.slot_of
  31.0 55.3 %grads.1 = (f32[8,64]{1,0:T(8,128)}, f32[8,16384]{1,0:T(8,128)}) custom-call(f32[3,16,16,256]{3,2,1,0:T(8,128)} %bitcast.9, f32[32,64]{1,0:T(8,128)} %compare_convert_fusion.chosen, f32[64,64]{1,0:T(8,128)} %fusion.6.slot_of, f32[32,16384]{1,0:T(8,128)} %stored_rows.1, f32[32,4096]{1,0:T(8,128)} %get-tuple-element.8.refs_0_, f32[32,4096]{1,0:T(8,128)} %get-tuple-element.9.refs_1_), custom_call_target="tpu_custom_call" | custom-call | tf_op jit(solution)/shard_map/grads/pallas_call | solution.py:389
  86.2 1.3 %copy.13 = f32[8,64]{1,0:T(8,128)} copy(f32[8,64]{1,0:T(8,128)} %get-tuple-element.22) | data formatting | bytes 4096
  87.5 1.9 %copy.14 = f32[8,16384]{1,0:T(8,128)} copy(f32[8,16384]{1,0:T(8,128)} %get-tuple-element.23) | data formatting | bytes 1048576
  (5 shorter events, 0.0 us)
Async XLA Ops:
  0.6 24.6 %copy-start = (f32[256,256]{1,0:T(8,128)S(1)}, f32[256,256]{1,0:T(8,128)}, u32[]{:S(2)}) copy-start(f32[256,256]{1,0:T(8,128)} %param.13) | copy-start | bytes 786436
  1.7 24.9 %copy-start.1 = (f32[256,256]{1,0:T(8,128)S(1)}, f32[256,256]{1,0:T(8,128)}, u32[]{:S(2)}) copy-start(f32[256,256]{1,0:T(8,128)} %param.14) | copy-start | bytes 786436
  1.7 27.9 %copy-start.2 = (s32[64]{0:T(128)S(1)}, s32[64]{0:T(128)}, u32[]{:S(2)}) copy-start(s32[64]{0:T(128)} %param.16) | copy-start | bytes 772

commit v4 on v3

--- a/solution.py
+++ b/solution.py
@@ -123,7 +123,7 @@
         copy.wait_send()
 
 
-def grads_kernel(sizes, part, chosen, slot_of, stored_rows, *refs):
+def grads_kernel(sizes, part, slots, stored_rows, *refs):
     feats, group_toks, groups, local, rows, spacing, pieces, early = sizes
     total, out = refs[early : early + 2]
     recv, grads, heads, picked, scored, landed, late = refs[early + 2 : early + 9]
@@ -240,47 +240,63 @@
         for way in range(2):
             if groups > 1:
                 each(way, 0, piece, "start", sending(way, 0))
-    for step in range(groups - 1):
+    seqs = grads.shape[1]
+    row = lax.broadcasted_iota(jnp.int32, (held, seqs), 0) + group * held
+    pick = jnp.where(slots[...] == row, 1.0, 0.0).astype(jnp.float32)
+    wide = height * rank
+    part_wide = tall * rank
+    first_lane = pl.multiple_of(spot * wide, wide)
+    score = jnp.zeros((group_toks * late.shape[1], seqs), jnp.float32)
+
+    def finish(piece, score):
+        lines = range(piece * tall, (piece + 1) * tall)
+        for at in range(1, groups):
+            span = pl.ds(piece * tall, tall)
+            grads[span, at * held - 1, :] += heads[at, span, :]
+        for line in lines:
+            lane = pl.ds(line * rank, rank)
+            taken = jnp.dot(
+                pick, grads[line], precision=highest, preferred_element_type=jnp.float32
+            )
+            for q in range(group_toks):
+                picked[q, :, lane] = taken[q * local : (q + 1) * local]
+        lanes = pl.ds(piece * part_wide, part_wide)
+        mine = pl.ds(pl.multiple_of(first_lane + piece * part_wide, part_wide), part_wide)
+        for step in range(1, group_toks):
+            to = (spot + step) % group_toks
+            trades.append(remote(
+                picked.at[to, :, lanes], out.at[:, mine],
+                psend.at[piece, step], precv.at[piece, step],
+                group * group_toks + to, feat,
+            ))
+            trades[-1].start()
+        out[:, mine] = picked[spot, :, lanes]
+        if piece == 0:
+            kept.wait()
+            for copy in trades[: group_toks - 1 - early]:
+                copy.wait_recv()
+        for line in lines:
+            lane = pl.ds(line * rank, rank)
+            block_rows = jnp.concatenate([ref[:, lane] for ref in stored], axis=0)
+            score += lax.dot_general(
+                block_rows, grads[line], (((1,), (1,)), ((), ())),
+                precision=highest, preferred_element_type=jnp.float32,
+            )
+        return score
+
+    for step in range(max(groups - 1, 1)):
         for piece in range(pieces):
-            for way in range(2):
-                each(way, step, piece, "wait_recv", taking(way, step))
-                if step + 1 < groups - 1:
-                    each(way, step + 1, piece, "start", sending(way, step + 1))
-    for step in range(groups - 1):
-        for piece in range(pieces):
-            for way in range(2):
-                each(way, step, piece, "wait_send", sending(way, step))
-
-    for at in range(1, groups):
-        grads[:, at * held - 1, :] += heads[at]
-    pick = chosen[...]
-    for line in range(height):
-        lane = pl.ds(line * rank, rank)
-        taken = jnp.dot(pick, grads[line], precision=highest, preferred_element_type=jnp.float32)
-        for q in range(group_toks):
-            picked[q, :, lane] = taken[q * local : (q + 1) * local]
-    wide = height * rank
-    mine = pl.ds(pl.multiple_of(spot * wide, wide), wide)
-    for step in range(1, group_toks):
-        to = (spot + step) % group_toks
-        trades.append(remote(
-            picked.at[to], out.at[:, mine], psend.at[step], precv.at[step],
-            group * group_toks + to, feat,
-        ))
-        trades[-1].start()
-    out[:, mine] = picked[spot]
-
-    kept.wait()
-    for copy in trades[: group_toks - 1 - early]:
-        copy.wait_recv()
-    score = jnp.zeros((group_toks * late.shape[1], grads.shape[1]), jnp.float32)
-    for line in range(height):
-        lane = pl.ds(line * rank, rank)
-        lanes = jnp.concatenate([ref[:, lane] for ref in stored], axis=0)
-        score += lax.dot_general(
-            lanes, grads[line], (((1,), (1,)), ((), ())),
-            precision=highest, preferred_element_type=jnp.float32,
-        )
+            if groups > 1:
+                for way in range(2):
+                    each(way, step, piece, "wait_recv", taking(way, step))
+                    if step + 1 < groups - 1:
+                        each(way, step + 1, piece, "start", sending(way, step + 1))
+            if step >= groups - 2:
+                for way in range(2):
+                    for sent in range(groups - 1):
+                        each(way, sent, piece, "wait_send", sending(way, sent))
+                score = finish(piece, score)
+
     scored[...] = jnp.zeros_like(scored)
     few = scored.shape[2]
     for step in range(group_toks):
@@ -302,9 +318,11 @@
     for number, copy in enumerate(parts, 1):
         copy.wait_recv()
         summed += landed[number // feats, number % feats]
-    total[...] = jnp.dot(
-        summed[:, : score.shape[1]], slot_of[...], precision=highest,
-        preferred_element_type=jnp.float32,
+    column = lax.broadcasted_iota(jnp.int32, (seqs, seqs), 0)
+    by_slot = jnp.where(slots[...] == column, 1.0, 0.0).astype(jnp.float32)
+    total[...] = lax.dot_general(
+        summed[:, :seqs], by_slot, (((1,), (1,)), ((), ())),
+        precision=highest, preferred_element_type=jnp.float32,
     )
     for copy in trades[group_toks - 1 - early :]:
         copy.wait_recv()
@@ -342,7 +360,7 @@
     store_rows, width = stored_grads.shape
     wide = width // group_toks
 
-    early = max(group_toks - 2, 1)
+    early = group_toks - 1
     any_space = pl.BlockSpec(memory_space=pl.ANY)
     lefts, mats = (out_grads, activations), (proj_out, proj_in)
     pair_rows = pltpu.VMEM((chips, rows, rank), f32)
@@ -377,22 +395,18 @@
     spread = jnp.concatenate([weights[:, k : k + 1] * left_side for k in range(near)], axis=1)
     part = lax.dot_general(spread, right_side, (((0,), (0,)), ((), ())), precision=highest)
 
-    held = group_toks * local
-    slots = (tok // group_toks) * held + jnp.arange(held, dtype=jnp.int32)
-    chosen = (slots[:, None] == seq_slots[None, :]).astype(f32)
     score_rows = store_rows // feats
     lanes = seq_count + -seq_count % 128
     pieces = 2 if height % 16 == 0 else 1
     hops = max(groups - 1, 1)
     sizes_ = (feats, group_toks, groups, local, rows, spacing, pieces, early)
-    slot_of = (seq_slots[:, None] == numbers[None, :]).astype(f32)
     scores, own_rows = pl.pallas_call(
         functools.partial(grads_kernel, sizes_),
         out_shape=[
             jax.ShapeDtypeStruct((score_rows, seq_count), f32),
             jax.ShapeDtypeStruct((local, width), f32),
         ],
-        in_specs=[VMEM] * 3 + [any_space] + [VMEM] * early,
+        in_specs=[VMEM] * 2 + [any_space] + [VMEM] * early,
         out_specs=[VMEM] * 2,
         scratch_shapes=[
             pltpu.VMEM((count, near, height, rank), f32),
@@ -405,12 +419,12 @@
         ]
         + [dma((pieces, count))] * 2
         + [dma((2, hops, pieces))] * 4
-        + [dma((group_toks,))] * 2
+        + [dma((pieces, group_toks))] * 2
         + [dma((group_toks, feats))] * 2
         + [dma((group_toks - early,))] * 2,
         compiler_params=pltpu.CompilerParams(collective_id=1, has_side_effects=True),
         name="grads",
-    )(part.reshape(near, count, height, rank), chosen, slot_of, stored_grads, *traded)
+    )(part.reshape(near, count, height, rank), seq_slots.reshape(1, seq_count), stored_grads, *traded)
     return scores, own_rows
 
 

time: 89.7 us -> 87.4 us (0.974)
  other arithmetic: 2.36 us -> 0.99 us
  Pallas kernels: 78.8 us -> 77.9 us
    pallas_call x1, Pallas kernels: 55.3 us -> 48.6 us  [body(): pl.pallas_call(functools.partial(grads_kernel, sizes_), out_shape=[jax.Sh...]
    pallas_call x1, Pallas kernels: 23.5 us -> 29.3 us  [body(): pl.pallas_call(functools.partial(project_kernel, (chips, rows, group_toks...]
    convert_element_type x2 -> x0, other arithmetic: 1.36 us -> none  [the longest x1 0.69 us: body(): slot_of = (seq_slots[:, None] == numbers[None, :]).astype(f32)]
    unnamed x8 -> x6, local copies, waits for them, and re-layouts: 3.16 us -> 3.15 us
where the time goes in v4:
time: 87.4 us; the launch traced here: 87.1 us
  Pallas kernels  77.9 us (89%)
  matrix products  4.37 us (5%)
  local copies, waits for them, and re-layouts  3.16 us (4%)
  other arithmetic  0.99 us (1%)
    pallas_call x1, Pallas kernels, body(): pl.pallas_call(functools.partial(grads_kernel, sizes_), out_shape=[jax.Sh...  48.6 us
    pallas_call x1, Pallas kernels, body(): pl.pallas_call(functools.partial(project_kernel, (chips, rows, group_toks...  29.3 us
    unnamed x6, local copies, waits for them, and re-layouts  3.15 us

profile of v4, /device:TPU:0, one launch (start us, length us, event | category | flops | bytes accessed | tf_op | source)
XLA Modules:
  0.0 87.1 jit_solution(5574784911934536213)
XLA Ops:
  0.6 0.0 copy-start
  0.7 0.9 %select_reduce_fusion.1 = (s32[3]{0:T(128)S(1)}, s32[3]{0:T(128)S(1)}) fusion(s32[64]{0:T(128)} %param.15, s32[3]{0:T(128)S(1)} %iota_add_fusion.1), kind=kLoop, calls=%fused_computation.12 | loop fusion | flops 1146 | bytes 292 | tf_op jit(solution)/shard_map/reduce_sum | solution.py:391
  1.6 0.1 convert_divide_fusion
  1.7 0.0 copy-start.1
  1.7 29.3 %project.1 = (f32[256,256]{1,0:T(8,128)}, f32[256,256]{1,0:T(8,128)}, f32[32,4096]{1,0:T(8,128)}, f32[32,4096]{1,0:T(8,128)}, f32[32,4096]{1,0:T(8,128)}) custom-call(bf16[1024,2048]{1,0:T(8,128)(2,1)} %refs_0_.1, bf16[1024,7168]{1,0:T(8,128)(2,1)} %refs_1_.1, bf16[2048,256]{1,0:T(8,128)(2,1)} %refs_2_.1, bf16[7168,256]{1,0:T(8,128)(2,1)} %refs_3_.1, ...), custom_call_target="tpu_custom_call" | custom-call | tf_op jit(solution)/shard_map/project/pallas_call | solution.py:367
  31.0 0.0 copy-done.1
  31.0 1.3 %fusion.9 = f32[256,256]{1,0:T(8,128)S(1)} fusion(f32[256,256]{1,0:T(8,128)} %get-tuple-element.8, f32[256,256]{1,0:T(8,128)S(1)} %copy-done.1), kind=kOutput, calls=%fused_computation.20 | convolution fusion | flops 201326592 | bytes 786432 | tf_op jit(solution)/shard_map/dot_general | solution.py:385
  32.4 0.0 copy-done
  32.4 1.4 %broadcast_multiply_fusion.2 = (f32[256,256]{0,1:T(8,128)S(1)}, f32[256,256]{0,1:T(8,128)S(1)}, f32[256,256]{0,1:T(8,128)S(1)}) fusion(f32[256]{0:T(256)S(1)} %bitcast.11, f32[256]{0:T(256)S(1)} %bitcast.12, f32[256]{0:T(256)S(1)} %bitcast.13, f32[256,256]{1,0:T(8,128)} %get-tuple-element.7, f32[256,256]{1,0:T(8,128)S(1)} %copy-done), kind=kOutput, calls=%fused_computation.8 | convolution fusion | flops 201523200 | bytes 1313792 | tf_op jit(solution)/shard_map/dot_general | solution.py:386
  33.8 1.7 %fusion = f32[768,256]{1,0:T(8,128)} fusion(f32[256,256]{1,0:T(8,128)S(1)} %fusion.9, f32[256,256]{0,1:T(8,128)S(1)} %get-tuple-element.15, f32[256,256]{0,1:T(8,128)S(1)} %get-tuple-element.16, f32[256,256]{0,1:T(8,128)S(1)} %get-tuple-element.14), kind=kOutput, calls=%fused_computation | convolution fusion | flops 604372992 | bytes 1835008 | tf_op jit(solution)/shard_map/dot_general | solution.py:396
  35.4 48.6 %grads.1 = (f32[8,64]{1,0:T(8,128)}, f32[8,16384]{1,0:T(8,128)}) custom-call(f32[3,16,16,256]{3,2,1,0:T(8,128)} %bitcast.10, s32[1,64]{1,0:T(1,128)} %bitcast.14, f32[32,16384]{1,0:T(8,128)} %stored_rows.1, f32[32,4096]{1,0:T(8,128)} %get-tuple-element.9.refs_0_, f32[32,4096]{1,0:T(8,128)} %get-tuple-element.10.refs_1_, f32[32,4096]{1,0:T(8,128)} %get-tuple-element.11.refs_2_), custom_call_target="tpu_custom_call" | custom-call | tf_op jit(solution)/shard_map/grads/pallas_call | solution.py:403
  84.0 1.3 %copy.13 = f32[8,64]{1,0:T(8,128)} copy(f32[8,64]{1,0:T(8,128)} %get-tuple-element.24) | data formatting | bytes 4096
  85.3 1.9 %copy.14 = f32[8,16384]{1,0:T(8,128)} copy(f32[8,16384]{1,0:T(8,128)} %get-tuple-element.25) | data formatting | bytes 1048576
  (4 shorter events, 0.0 us)
Async XLA Ops:
  0.6 31.8 %copy-start = (f32[256,256]{1,0:T(8,128)S(1)}, f32[256,256]{1,0:T(8,128)}, u32[]{:S(2)}) copy-start(f32[256,256]{1,0:T(8,128)} %param.13) | copy-start | bytes 786436
  1.7 29.4 %copy-start.1 = (f32[256,256]{1,0:T(8,128)S(1)}, f32[256,256]{1,0:T(8,128)}, u32[]{:S(2)}) copy-start(f32[256,256]{1,0:T(8,128)} %param.14) | copy-start | bytes 786436

commit v5 on v4

--- a/solution.py
+++ b/solution.py
@@ -177,14 +177,6 @@
     )
     kept.start()
     trades = []
-    for step in range(early + 1, group_toks):
-        to = (spot + step) % group_toks
-        trades.append(remote(
-            stored_rows.at[:, pl.ds(pl.multiple_of(to * width, width), width)],
-            late.at[step - early], lsend.at[step - early], lrecv.at[step - early],
-            group * group_toks + to, feat,
-        ))
-        trades[-1].start()
     stored = [late.at[0], *refs[:early]] + [
         late.at[step - early] for step in range(early + 1, group_toks)
     ]
@@ -240,6 +232,14 @@
         for way in range(2):
             if groups > 1:
                 each(way, 0, piece, "start", sending(way, 0))
+    for step in range(early + 1, group_toks):
+        to = (spot + step) % group_toks
+        trades.append(remote(
+            stored_rows.at[:, pl.ds(pl.multiple_of(to * width, width), width)],
+            late.at[step - early], lsend.at[step - early], lrecv.at[step - early],
+            group * group_toks + to, feat,
+        ))
+        trades[-1].start()
     seqs = grads.shape[1]
     row = lax.broadcasted_iota(jnp.int32, (held, seqs), 0) + group * held
     pick = jnp.where(slots[...] == row, 1.0, 0.0).astype(jnp.float32)
@@ -360,7 +360,7 @@
     store_rows, width = stored_grads.shape
     wide = width // group_toks
 
-    early = group_toks - 1
+    early = group_toks - 2
     any_space = pl.BlockSpec(memory_space=pl.ANY)
     lefts, mats = (out_grads, activations), (proj_out, proj_in)
     pair_rows = pltpu.VMEM((chips, rows, rank), f32)

time: 87.4 us -> 87 us (level)
    pallas_call x1, Pallas kernels: 29.3 us -> 23.5 us  [body(): pl.pallas_call(functools.partial(project_kernel, (chips, rows, group_toks...]
    pallas_call x1, Pallas kernels: 48.6 us -> 53.6 us  [body(): pl.pallas_call(functools.partial(grads_kernel, sizes_), out_shape=[jax.Sh...]
where the time goes in v5:
time: 87 us; the launch traced here: 86.3 us
  Pallas kernels  77.1 us (89%)
  matrix products  4.38 us (5%)
  local copies, waits for them, and re-layouts  3.14 us (4%)
  other arithmetic  0.99 us (1%)
    pallas_call x1, Pallas kernels, body(): pl.pallas_call(functools.partial(grads_kernel, sizes_), out_shape=[jax.Sh...  53.6 us
    pallas_call x1, Pallas kernels, body(): pl.pallas_call(functools.partial(project_kernel, (chips, rows, group_toks...  23.5 us
    unnamed x6, local copies, waits for them, and re-layouts  3.14 us

profile of v5, /device:TPU:0, one launch (start us, length us, event | category | flops | bytes accessed | tf_op | source)
XLA Modules:
  0.0 86.3 jit_solution(8922665770513895169)
XLA Ops:
  0.6 0.0 copy-start
  0.7 0.9 %select_reduce_fusion.1 = (s32[3]{0:T(128)S(1)}, s32[3]{0:T(128)S(1)}) fusion(s32[64]{0:T(128)} %param.15, s32[3]{0:T(128)S(1)} %iota_add_fusion.1), kind=kLoop, calls=%fused_computation.12 | loop fusion | flops 1146 | bytes 292 | tf_op jit(solution)/shard_map/reduce_sum | solution.py:391
  1.6 0.1 convert_divide_fusion
  1.7 0.0 copy-start.1
  1.7 23.5 %project.1 = (f32[256,256]{1,0:T(8,128)}, f32[256,256]{1,0:T(8,128)}, f32[32,4096]{1,0:T(8,128)}, f32[32,4096]{1,0:T(8,128)}) custom-call(bf16[1024,2048]{1,0:T(8,128)(2,1)} %refs_0_.1, bf16[1024,7168]{1,0:T(8,128)(2,1)} %refs_1_.1, bf16[2048,256]{1,0:T(8,128)(2,1)} %refs_2_.1, bf16[7168,256]{1,0:T(8,128)(2,1)} %refs_3_.1, f32[32,16384]{1,0:T(8,128)} %stored_rows.1), custom_call_target="tpu_custom_call" | custom-call | tf_op jit(solution)/shard_map/project/pallas_call | solution.py:367
  25.2 0.0 copy-done.1
  25.2 1.3 %fusion.9 = f32[256,256]{1,0:T(8,128)S(1)} fusion(f32[256,256]{1,0:T(8,128)} %get-tuple-element.7, f32[256,256]{1,0:T(8,128)S(1)} %copy-done.1), kind=kOutput, calls=%fused_computation.20 | convolution fusion | flops 201326592 | bytes 786432 | tf_op jit(solution)/shard_map/dot_general | solution.py:385
  26.5 0.0 copy-done
  26.5 1.4 %broadcast_multiply_fusion.2 = (f32[256,256]{0,1:T(8,128)S(1)}, f32[256,256]{0,1:T(8,128)S(1)}, f32[256,256]{0,1:T(8,128)S(1)}) fusion(f32[256]{0:T(256)S(1)} %bitcast.11, f32[256]{0:T(256)S(1)} %bitcast.12, f32[256]{0:T(256)S(1)} %bitcast.13, f32[256,256]{1,0:T(8,128)} %get-tuple-element.6, f32[256,256]{1,0:T(8,128)S(1)} %copy-done), kind=kOutput, calls=%fused_computation.8 | convolution fusion | flops 201523200 | bytes 1313792 | tf_op jit(solution)/shard_map/dot_general | solution.py:386
  27.9 1.7 %fusion = f32[768,256]{1,0:T(8,128)} fusion(f32[256,256]{1,0:T(8,128)S(1)} %fusion.9, f32[256,256]{0,1:T(8,128)S(1)} %get-tuple-element.13, f32[256,256]{0,1:T(8,128)S(1)} %get-tuple-element.14, f32[256,256]{0,1:T(8,128)S(1)} %get-tuple-element.12), kind=kOutput, calls=%fused_computation | convolution fusion | flops 604372992 | bytes 1835008 | tf_op jit(solution)/shard_map/dot_general | solution.py:396
  29.6 53.6 %grads.1 = (f32[8,64]{1,0:T(8,128)}, f32[8,16384]{1,0:T(8,128)}) custom-call(f32[3,16,16,256]{3,2,1,0:T(8,128)} %bitcast.10, s32[1,64]{1,0:T(1,128)} %bitcast.14, f32[32,16384]{1,0:T(8,128)} %stored_rows.1, f32[32,4096]{1,0:T(8,128)} %get-tuple-element.8.refs_0_, f32[32,4096]{1,0:T(8,128)} %get-tuple-element.9.refs_1_), custom_call_target="tpu_custom_call" | custom-call | tf_op jit(solution)/shard_map/grads/pallas_call | solution.py:403
  83.2 1.3 %copy.13 = f32[8,64]{1,0:T(8,128)} copy(f32[8,64]{1,0:T(8,128)} %get-tuple-element.22) | data formatting | bytes 4096
  84.4 1.9 %copy.14 = f32[8,16384]{1,0:T(8,128)} copy(f32[8,16384]{1,0:T(8,128)} %get-tuple-element.23) | data formatting | bytes 1048576
  (4 shorter events, 0.0 us)
Async XLA Ops:
  0.6 25.9 %copy-start = (f32[256,256]{1,0:T(8,128)S(1)}, f32[256,256]{1,0:T(8,128)}, u32[]{:S(2)}) copy-start(f32[256,256]{1,0:T(8,128)} %param.13) | copy-start | bytes 786436
  1.7 23.5 %copy-start.1 = (f32[256,256]{1,0:T(8,128)S(1)}, f32[256,256]{1,0:T(8,128)}, u32[]{:S(2)}) copy-start(f32[256,256]{1,0:T(8,128)} %param.14) | copy-start | bytes 786436
